TPU v7x, 32 devices: a whole 2x2x4 slice. The times are simulated.
32 devices in a mesh: dp: 2 (over core), ctx: 4 (over z), tp: 4 (over y, x).
Axes of the slice: x: 2, y: 2, z: 4, core: 2. Of those that a mesh axis runs over, the one named last changes fastest.
Arguments:
- block_input: float32 [512, 2, 1024], P(('ctx', 'tp'), 'dp'), may hold values from -6 to 6
- input_gain: float32 [2, 1024], replicated, may hold values from 0.5 to 1.5
- query_weight: bfloat16 [2, 1024, 2048], P(None, None, 'tp'), may hold values from -0.1875 to 0.1875
- key_weight: bfloat16 [2, 1024, 1024], P(None, None, 'tp'), may hold values from -0.1875 to 0.1875
- value_weight: bfloat16 [2, 1024, 1024], P(None, None, 'tp'), may hold values from -0.1875 to 0.1875
- query_gain: float32 [2, 128], replicated, may hold values from 0.1 to 1.9
- key_gain: float32 [2, 128], replicated, may hold values from 0.1 to 1.9
- out_weight: bfloat16 [2, 2048, 1024], P(None, 'tp'), may hold values from -0.75 to 0.75
- post_gain: float32 [2, 1024], replicated, may hold values from 0.5 to 1.5
- gate_weight: bfloat16 [2, 1024, 3072], P(None, None, 'tp'), may hold values from -0.1875 to 0.1875
- up_weight: bfloat16 [2, 1024, 3072], P(None, None, 'tp'), may hold values from -0.1875 to 0.1875
- down_weight: bfloat16 [2, 3072, 1024], P(None, 'tp'), may hold values from -0.109375 to 0.109375
- grad_output: float32 [512, 2, 1024], P(('ctx', 'tp'), 'dp'), may hold values from -6 to 6
Outputs:
- output: float32 [512, 2, 1024], P(('ctx', 'tp'), 'dp')
- grad_input: float32 [512, 2, 1024], P(('ctx', 'tp'), 'dp')
- input_gain_grad: float32 [2, 1024], replicated
- query_weight_grad: float32 [2, 1024, 2048], P(None, ('dp', 'ctx'), 'tp')
- key_weight_grad: float32 [2, 1024, 1024], P(None, ('dp', 'ctx'), 'tp')
- value_weight_grad: float32 [2, 1024, 1024], P(None, ('dp', 'ctx'), 'tp')
- query_gain_grad: float32 [2, 128], replicated
- key_gain_grad: float32 [2, 128], replicated
- out_weight_grad: float32 [2, 2048, 1024], P(None, 'tp', ('dp', 'ctx'))
- post_gain_grad: float32 [2, 1024], replicated
- gate_weight_grad: float32 [2, 1024, 3072], P(None, ('dp', 'ctx'), 'tp')
- up_weight_grad: float32 [2, 1024, 3072], P(None, ('dp', 'ctx'), 'tp')
- down_weight_grad: float32 [2, 3072, 1024], P(None, 'tp', ('dp', 'ctx'))
All inputs are finite; a program needn't handle non-finite values.
Results may differ from a plain program's by a relative error of at most 0.034.
Values may be sent and summed in bfloat16 or wider, within the bound.
A program may use at most 192 MiB of HBM per device.

v0:
```python
import jax
import jax.numpy as jnp
from jax import lax
from jax.sharding import PartitionSpec as P

EPS = 1e-06
THETA = 1000000.0


def rms_forward(field, gain):
    inverse = lax.rsqrt(jnp.mean(field * field, axis=-1, keepdims=True) + EPS)
    normed = field * inverse
    return (normed * gain, normed, inverse)


def rms_backward(grad_out, normed, inverse, gain):
    leading = tuple(range(grad_out.ndim - 1))
    grad_gain = jnp.sum(grad_out * normed, axis=leading)
    scaled = grad_out * gain
    grad_in = inverse * (scaled - normed * jnp.mean(scaled * normed, axis=-1, keepdims=True))
    return (grad_in, grad_gain)


def rope_tables(positions, head_dim):
    half = head_dim // 2
    frequency = THETA ** (-(2.0 * jnp.arange(half, dtype=jnp.float32)) / head_dim)
    angles = positions[:, None] * frequency[None, :]
    angles = jnp.concatenate([angles, angles], axis=-1)
    return (jnp.cos(angles)[:, None, None, :], jnp.sin(angles)[:, None, None, :])


def rotate(field, cosine, sine):
    half = field.shape[-1] // 2
    turned = jnp.concatenate([-field[..., half:], field[..., :half]], axis=-1)
    return field * cosine + turned * sine


def on_device(
    block_input,
    input_gain,
    query_weight,
    key_weight,
    value_weight,
    query_gain,
    key_gain,
    out_weight,
    post_gain,
    gate_weight,
    up_weight,
    down_weight,
    grad_output,
):
    local_rows, seq_local, model_width = block_input.shape
    layer_count = input_gain.shape[0]
    head_dim = query_gain.shape[-1]
    heads_local = query_weight.shape[-1] // head_dim
    kv_local = key_weight.shape[-1] // head_dim
    group_size = heads_local // kv_local
    block_rows = local_rows * lax.axis_size("tp")
    total_rows = block_rows * lax.axis_size("ctx")
    score_scale = head_dim ** (-0.5)
    first_row = lax.axis_index("ctx") * block_rows
    last_row = first_row + block_rows - 1
    query_rows = first_row + jnp.arange(block_rows, dtype=jnp.int32)
    cosine, sine = rope_tables(query_rows.astype(jnp.float32), head_dim)
    grouped_shape = (block_rows, seq_local, kv_local, group_size, head_dim)

    def piece_scores(query_grouped, key_piece):
        count = key_piece.shape[0]
        scores = (
            jnp.einsum(
                "qskgd,tskd->skgqt", query_grouped, key_piece, preferred_element_type=jnp.float32
            )
            * score_scale
        )
        key_rows = jnp.arange(count, dtype=jnp.int32)
        return jnp.where(key_rows[None, :] <= query_rows[:, None], scores, -jnp.inf)

    hidden = block_input
    kept_all = []
    for index in range(layer_count):
        normed_one, forward_plain_one, forward_inverse_one = rms_forward(hidden, input_gain[index])
        forward_gathered = lax.all_gather(normed_one.astype(jnp.bfloat16), "tp", axis=0, tiled=True)
        query = jnp.einsum(
            "rsd,dh->rsh", forward_gathered, query_weight[index], preferred_element_type=jnp.float32
        )
        keys = jnp.einsum(
            "rsd,dh->rsh", forward_gathered, key_weight[index], preferred_element_type=jnp.float32
        )
        forward_value_bf = jnp.einsum(
            "rsd,dh->rsh", forward_gathered, value_weight[index], preferred_element_type=jnp.float32
        ).astype(jnp.bfloat16)
        query_normed, forward_query_plain, forward_query_inverse = rms_forward(
            query.reshape(block_rows, seq_local, heads_local, head_dim), query_gain[index]
        )
        key_normed, forward_key_plain, forward_key_inverse = rms_forward(
            keys.reshape(block_rows, seq_local, kv_local, head_dim), key_gain[index]
        )
        forward_query_grouped = (
            rotate(query_normed, cosine, sine).astype(jnp.bfloat16).reshape(grouped_shape)
        )
        forward_key_rot = (
            rotate(key_normed, cosine, sine)
            .astype(jnp.bfloat16)
            .reshape(block_rows, seq_local, kv_local * head_dim)
        )
        stat_shape = (seq_local, kv_local, group_size, block_rows)
        forward_initial = (
            jnp.full(stat_shape, -1e30, jnp.float32),
            jnp.zeros(stat_shape, jnp.float32),
            jnp.zeros(grouped_shape, jnp.float32),
        )
        pieces = (
            lax.all_gather(forward_key_rot, "ctx", axis=0, tiled=True),
            lax.all_gather(forward_value_bf, "ctx", axis=0, tiled=True),
        )

        def update(state):
            running, totals, accum = state
            count = pieces[0].shape[0]
            key_piece = pieces[0].reshape(count, seq_local, kv_local, head_dim)
            value_piece = pieces[1].reshape(count, seq_local, kv_local, head_dim)
            scores = piece_scores(forward_query_grouped, key_piece)
            newest = jnp.maximum(running, jnp.max(scores, axis=-1))
            factor = jnp.exp(running - newest)
            weights = jnp.exp(scores - newest[..., None])
            totals = jnp.sum(weights, axis=-1)
            mixed = jnp.einsum(
                "skgqt,tskd->qskgd",
                weights.astype(jnp.bfloat16),
                value_piece,
                preferred_element_type=jnp.float32,
            )
            accum = accum * jnp.moveaxis(factor, 3, 0)[..., None] + mixed
            return (newest, totals, accum)

        running, totals, accum = lax.cond(
            jnp.int32(0) <= last_row, update, lambda state: state, forward_initial
        )
        attended = accum / jnp.moveaxis(totals, 3, 0)[..., None]
        forward_log_total = running + jnp.log(totals)
        forward_heads_bf = attended.reshape(block_rows, seq_local, heads_local * head_dim).astype(
            jnp.bfloat16
        )
        mixed = hidden + lax.psum_scatter(
            jnp.einsum(
                "rsh,hd->rsd",
                forward_heads_bf,
                out_weight[index],
                preferred_element_type=jnp.float32,
            ).astype(jnp.bfloat16),
            "tp",
            scatter_dimension=0,
            tiled=True,
        ).astype(jnp.float32)
        normed_two, forward_plain_two, forward_inverse_two = rms_forward(mixed, post_gain[index])
        forward_gathered_two = lax.all_gather(
            normed_two.astype(jnp.bfloat16), "tp", axis=0, tiled=True
        )
        forward_gate = jnp.einsum(
            "rsd,df->rsf",
            forward_gathered_two,
            gate_weight[index],
            preferred_element_type=jnp.float32,
        )
        forward_upward = jnp.einsum(
            "rsd,df->rsf",
            forward_gathered_two,
            up_weight[index],
            preferred_element_type=jnp.float32,
        )
        forward_swish = (jax.nn.silu(forward_gate) * forward_upward).astype(jnp.bfloat16)
        result = mixed + lax.psum_scatter(
            jnp.einsum(
                "rsf,fd->rsd", forward_swish, down_weight[index], preferred_element_type=jnp.float32
            ).astype(jnp.bfloat16),
            "tp",
            scatter_dimension=0,
            tiled=True,
        ).astype(jnp.float32)
        forward_kept = (
            forward_plain_one,
            forward_inverse_one,
            forward_gathered,
            forward_query_plain,
            forward_query_inverse,
            forward_key_plain,
            forward_key_inverse,
            forward_query_grouped,
            forward_key_rot,
            forward_value_bf,
            forward_log_total,
            forward_heads_bf,
            forward_plain_two,
            forward_inverse_two,
            forward_gathered_two,
            forward_gate,
            forward_upward,
            forward_swish,
        )
        hidden = result
        kept_all.append(forward_kept)
    grad_hidden = grad_output
    weight_parts = [None] * layer_count
    gain_parts = [None] * layer_count
    for index in reversed(range(layer_count)):
        backward_kept = kept_all[index]
        (
            plain_one,
            inverse_one,
            gathered,
            query_plain,
            query_inverse,
            key_plain,
            key_inverse,
            backward_query_grouped,
            key_rot,
            value_bf,
            log_total,
            heads_bf,
            plain_two,
            inverse_two,
            gathered_two,
            gate,
            upward,
            swish,
        ) = backward_kept
        grad_rows = lax.all_gather(grad_hidden.astype(jnp.bfloat16), "tp", axis=0, tiled=True)
        grad_swish = jnp.einsum(
            "rsd,fd->rsf", grad_rows, down_weight[index], preferred_element_type=jnp.float32
        )
        down_grad = jnp.einsum("rsf,rsd->fd", swish, grad_rows, preferred_element_type=jnp.float32)
        sigma = jax.nn.sigmoid(gate)
        grad_gate = (grad_swish * upward * (sigma * (1.0 + gate * (1.0 - sigma)))).astype(
            jnp.bfloat16
        )
        grad_up = (grad_swish * (gate * sigma)).astype(jnp.bfloat16)
        gate_grad = jnp.einsum(
            "rsd,rsf->df", gathered_two, grad_gate, preferred_element_type=jnp.float32
        )
        up_grad = jnp.einsum(
            "rsd,rsf->df", gathered_two, grad_up, preferred_element_type=jnp.float32
        )
        grad_second = lax.psum_scatter(
            (
                jnp.einsum(
                    "rsf,df->rsd", grad_gate, gate_weight[index], preferred_element_type=jnp.float32
                )
                + jnp.einsum(
                    "rsf,df->rsd", grad_up, up_weight[index], preferred_element_type=jnp.float32
                )
            ).astype(jnp.bfloat16),
            "tp",
            scatter_dimension=0,
            tiled=True,
        ).astype(jnp.float32)
        grad_norm_two, post_part = rms_backward(
            grad_second, plain_two, inverse_two, post_gain[index]
        )
        grad_mixed = grad_hidden + grad_norm_two
        mixed_rows = lax.all_gather(grad_mixed.astype(jnp.bfloat16), "tp", axis=0, tiled=True)
        grad_heads = jnp.einsum(
            "rsd,hd->rsh", mixed_rows, out_weight[index], preferred_element_type=jnp.float32
        ).astype(jnp.bfloat16)
        out_grad = jnp.einsum(
            "rsh,rsd->hd", heads_bf, mixed_rows, preferred_element_type=jnp.float32
        )
        grad_grouped = grad_heads.reshape(grouped_shape)
        heads_grouped = heads_bf.reshape(grouped_shape)
        delta = jnp.moveaxis(
            jnp.sum(grad_grouped.astype(jnp.float32) * heads_grouped.astype(jnp.float32), axis=-1),
            0,
            3,
        )

        def block_terms(key_flat, value_flat):
            count = key_flat.shape[0]
            key_piece = key_flat.reshape(count, seq_local, kv_local, head_dim)
            value_piece = value_flat.reshape(count, seq_local, kv_local, head_dim)
            scores = piece_scores(backward_query_grouped, key_piece)
            probs = jnp.exp(scores - log_total[..., None])
            dprob = jnp.einsum(
                "qskgd,tskd->skgqt", grad_grouped, value_piece, preferred_element_type=jnp.float32
            )
            dscore = (probs * (dprob - delta[..., None])).astype(jnp.bfloat16)
            query_term = (
                jnp.einsum(
                    "skgqt,tskd->qskgd", dscore, key_piece, preferred_element_type=jnp.float32
                )
                * score_scale
            )
            key_part = (
                jnp.einsum(
                    "skgqt,qskgd->tskd",
                    dscore,
                    backward_query_grouped,
                    preferred_element_type=jnp.float32,
                )
                * score_scale
            )
            value_part = jnp.einsum(
                "skgqt,qskgd->tskd",
                probs.astype(jnp.bfloat16),
                grad_grouped,
                preferred_element_type=jnp.float32,
            )
            flat_shape = (count, seq_local, kv_local * head_dim)
            return (query_term, key_part.reshape(flat_shape), value_part.reshape(flat_shape))

        sums_shape = (total_rows, seq_local, kv_local * head_dim)
        initial = (
            jnp.zeros(grouped_shape, jnp.float32),
            jnp.zeros(sums_shape, jnp.float32),
            jnp.zeros(sums_shape, jnp.float32),
        )
        absorb_pieces = (
            lax.all_gather(key_rot, "ctx", axis=0, tiled=True),
            lax.all_gather(value_bf, "ctx", axis=0, tiled=True),
        )

        def absorb_update(state):
            count = absorb_pieces[0].shape[0]
            query_term, key_term, value_term = block_terms(absorb_pieces[0], absorb_pieces[1])
            return (query_term, key_term, value_term)

        grad_query, key_sums, value_sums = lax.cond(
            jnp.int32(0) <= last_row, absorb_update, lambda state: state, initial
        )
        grad_keys = lax.psum_scatter(
            key_sums.astype(jnp.bfloat16), "ctx", scatter_dimension=0, tiled=True
        ).astype(jnp.float32)
        grad_values = lax.psum_scatter(
            value_sums.astype(jnp.bfloat16), "ctx", scatter_dimension=0, tiled=True
        )
        grad_query = rotate(
            grad_query.reshape(block_rows, seq_local, heads_local, head_dim), cosine, -sine
        )
        grad_keys = rotate(
            grad_keys.reshape(block_rows, seq_local, kv_local, head_dim), cosine, -sine
        )
        grad_query, query_part = rms_backward(
            grad_query, query_plain, query_inverse, query_gain[index]
        )
        grad_keys, key_part = rms_backward(grad_keys, key_plain, key_inverse, key_gain[index])
        query_bf = grad_query.reshape(block_rows, seq_local, heads_local * head_dim).astype(
            jnp.bfloat16
        )
        key_bf = grad_keys.reshape(block_rows, seq_local, kv_local * head_dim).astype(jnp.bfloat16)
        query_grad = jnp.einsum(
            "rsd,rsh->dh", gathered, query_bf, preferred_element_type=jnp.float32
        )
        key_grad = jnp.einsum("rsd,rsh->dh", gathered, key_bf, preferred_element_type=jnp.float32)
        value_grad = jnp.einsum(
            "rsd,rsh->dh", gathered, grad_values, preferred_element_type=jnp.float32
        )
        grad_first = lax.psum_scatter(
            (
                jnp.einsum(
                    "rsh,dh->rsd", query_bf, query_weight[index], preferred_element_type=jnp.float32
                )
                + jnp.einsum(
                    "rsh,dh->rsd", key_bf, key_weight[index], preferred_element_type=jnp.float32
                )
                + jnp.einsum(
                    "rsh,dh->rsd",
                    grad_values,
                    value_weight[index],
                    preferred_element_type=jnp.float32,
                )
            ).astype(jnp.bfloat16),
            "tp",
            scatter_dimension=0,
            tiled=True,
        ).astype(jnp.float32)
        grad_norm_one, input_part = rms_backward(
            grad_first, plain_one, inverse_one, input_gain[index]
        )
        grad_next = grad_mixed + grad_norm_one
        weight_grads = (query_grad, key_grad, value_grad, out_grad, gate_grad, up_grad, down_grad)
        gain_grads = (input_part, query_part, key_part, post_part)
        grad_hidden, weight_grads, gain_grads = (grad_next, weight_grads, gain_grads)
        weight_parts[index] = weight_grads
        gain_parts[index] = gain_grads
    stacked = [jnp.stack([part[member] for part in weight_parts]) for member in range(7)]
    stacked = (
        lax.psum_scatter(
            stacked[0].astype(jnp.bfloat16), ("dp", "ctx"), scatter_dimension=1, tiled=True
        ).astype(jnp.float32),
        lax.psum_scatter(
            stacked[1].astype(jnp.bfloat16), ("dp", "ctx"), scatter_dimension=1, tiled=True
        ).astype(jnp.float32),
        lax.psum_scatter(
            stacked[2].astype(jnp.bfloat16), ("dp", "ctx"), scatter_dimension=1, tiled=True
        ).astype(jnp.float32),
        lax.psum_scatter(
            stacked[3].astype(jnp.bfloat16), ("dp", "ctx"), scatter_dimension=2, tiled=True
        ).astype(jnp.float32),
        lax.psum_scatter(
            stacked[4].astype(jnp.bfloat16), ("dp", "ctx"), scatter_dimension=1, tiled=True
        ).astype(jnp.float32),
        lax.psum_scatter(
            stacked[5].astype(jnp.bfloat16), ("dp", "ctx"), scatter_dimension=1, tiled=True
        ).astype(jnp.float32),
        lax.psum_scatter(
            stacked[6].astype(jnp.bfloat16), ("dp", "ctx"), scatter_dimension=2, tiled=True
        ).astype(jnp.float32),
    )
    gains = [jnp.stack([part[member] for part in gain_parts]) for member in range(4)]
    gains = lax.psum((gains[0], gains[1], gains[2], gains[3]), ("dp", "ctx", "tp"))
    return (
        hidden,
        grad_hidden,
        gains[0],
        stacked[0],
        stacked[1],
        stacked[2],
        gains[1],
        gains[2],
        stacked[3],
        gains[3],
        stacked[4],
        stacked[5],
        stacked[6],
    )


def solution(mesh):
    placed = (
        P(("ctx", "tp"), "dp", None),
        P(),
        P(None, None, "tp"),
        P(None, None, "tp"),
        P(None, None, "tp"),
        P(),
        P(),
        P(None, "tp", None),
        P(),
        P(None, None, "tp"),
        P(None, None, "tp"),
        P(None, "tp", None),
        P(("ctx", "tp"), "dp", None),
    )
    return jax.shard_map(
        on_device,
        mesh=mesh,
        in_specs=placed,
        out_specs=(
            P(("ctx", "tp"), "dp", None),
            P(("ctx", "tp"), "dp", None),
            P(),
            P(None, ("dp", "ctx"), "tp"),
            P(None, ("dp", "ctx"), "tp"),
            P(None, ("dp", "ctx"), "tp"),
            P(),
            P(),
            P(None, "tp", ("dp", "ctx")),
            P(),
            P(None, ("dp", "ctx"), "tp"),
            P(None, ("dp", "ctx"), "tp"),
            P(None, "tp", ("dp", "ctx")),
        ),
        check_vma=False,
    )
```

profile of v0, /device:TPU:0, one launch (start us, length us, event | category | flops | bytes accessed | tf_op | source)
XLA Modules:
  0.0 907.1 jit_solution(9856992033902718018)
XLA Ops:
  10.3 10.5 %all_gather.40 = bf16[128,1,1024]{2,0,1:T(8,128)(2,1)S(1)} all-gather(bf16[32,1,1024]{2,0,1:T(8,128)(2,1)S(1)} %multiply_convert_fusion.9), channel_id=1, replica_groups=mesh['dp'=2,'ctx'=4,'tp'=4] {'tp'}, dimensions={0}, use_global_device_ids=true | all-gather | bytes 327680 | tf_op jit(solution)/shard_map/all_gather | solution.py:83
  24.8 14.7 %all-gather = bf16[512,256]{1,0:T(8,128)(2,1)S(1)} all-gather(bf16[128,256]{1,0:T(8,128)(2,1)S(1)} %fusion.265), channel_id=2, replica_groups=mesh['dp'=2,'ctx'=4,'tp'=4] {'ctx'}, dimensions={0}, use_global_device_ids=true | all-gather | bytes 327680 | tf_op jit(solution)/shard_map/all_gather | solution.py:114
  41.3 15.1 %all-gather.1 = bf16[512,256]{1,0:T(8,128)(2,1)} all-gather(bf16[128,256]{1,0:T(8,128)(2,1)S(1)} %convolution_convert_fusion.19), channel_id=3, replica_groups=mesh['dp'=2,'ctx'=4,'tp'=4] {'ctx'}, dimensions={0}, use_global_device_ids=true | all-gather | bytes 327680 | tf_op jit(solution)/shard_map/all_gather | solution.py:115
  65.1 23.3 %reduce-scatter.28.cloned.1.call-done = bf16[32,1,1024]{2,0,1:T(8,128)(2,1)} async-done(((bf16[128,1,1024]{2,0,1:T(8,128)(2,1)}), bf16[32,1,1024]{2,0,1:T(8,128)(2,1)}) %reduce-scatter.28.cloned.1.call-update) | async-done | bytes 65552 | tf_op jit(solution)/shard_map/reduce_scatter | solution.py:145
  89.7 9.3 %all_gather.43 = bf16[128,1,1024]{2,0,1:T(8,128)(2,1)S(1)} all-gather(bf16[32,1,1024]{2,0,1:T(8,128)(2,1)S(1)} %multiply_convert_fusion.8), channel_id=1, replica_groups=mesh['dp'=2,'ctx'=4,'tp'=4] {'tp'}, dimensions={0}, use_global_device_ids=true | all-gather | bytes 327680 | tf_op jit(solution)/shard_map/all_gather | solution.py:157
  104.9 24.4 %reduce-scatter.30.cloned.1.call-done = bf16[32,1,1024]{2,0,1:T(8,128)(2,1)} async-done(((bf16[128,1,1024]{2,0,1:T(8,128)(2,1)}), bf16[32,1,1024]{2,0,1:T(8,128)(2,1)}) %reduce-scatter.30.cloned.1.call-update) | async-done | bytes 65552 | tf_op jit(solution)/shard_map/reduce_scatter | solution.py:173
  131.2 9.3 %all_gather.44 = bf16[128,1,1024]{2,0,1:T(8,128)(2,1)S(1)} all-gather(bf16[32,1,1024]{2,0,1:T(8,128)(2,1)S(1)} %multiply_convert_fusion.7), channel_id=1, replica_groups=mesh['dp'=2,'ctx'=4,'tp'=4] {'tp'}, dimensions={0}, use_global_device_ids=true | all-gather | bytes 327680 | tf_op jit(solution)/shard_map/all_gather | solution.py:83
  145.3 14.3 %all-gather.2 = bf16[512,256]{1,0:T(8,128)(2,1)S(1)} all-gather(bf16[128,256]{1,0:T(8,128)(2,1)S(1)} %fusion.263), channel_id=4, replica_groups=mesh['dp'=2,'ctx'=4,'tp'=4] {'ctx'}, dimensions={0}, use_global_device_ids=true | all-gather | bytes 327680 | tf_op jit(solution)/shard_map/all_gather | solution.py:114
  160.0 13.8 %all-gather.3 = bf16[512,256]{1,0:T(8,128)(2,1)S(1)} all-gather(bf16[128,256]{1,0:T(8,128)(2,1)S(1)} %convolution_convert_fusion.18), channel_id=5, replica_groups=mesh['dp'=2,'ctx'=4,'tp'=4] {'ctx'}, dimensions={0}, use_global_device_ids=true | all-gather | bytes 327680 | tf_op jit(solution)/shard_map/all_gather | solution.py:115
  174.7 8.2 conditional.5
  197.1 13.8 %reduce-scatter.32.cloned.1.call-done = bf16[32,1,1024]{2,0,1:T(8,128)(2,1)} async-done(((bf16[128,1,1024]{2,0,1:T(8,128)(2,1)}), bf16[32,1,1024]{2,0,1:T(8,128)(2,1)}) %reduce-scatter.32.cloned.1.call-update) | async-done | bytes 65552 | tf_op jit(solution)/shard_map/reduce_scatter | solution.py:145
  212.6 9.4 %all_gather.47 = bf16[128,1,1024]{2,0,1:T(8,128)(2,1)S(1)} all-gather(bf16[32,1,1024]{2,0,1:T(8,128)(2,1)S(1)} %multiply_convert_fusion.6), channel_id=1, replica_groups=mesh['dp'=2,'ctx'=4,'tp'=4] {'tp'}, dimensions={0}, use_global_device_ids=true | all-gather | bytes 327680 | tf_op jit(solution)/shard_map/all_gather | solution.py:157
  232.5 20.4 %reduce-scatter.36.cloned.1.call-done = bf16[32,1,1024]{2,0,1:T(8,128)(2,1)} async-done(((bf16[128,1,1024]{2,0,1:T(8,128)(2,1)}), bf16[32,1,1024]{2,0,1:T(8,128)(2,1)}) %reduce-scatter.36.cloned.1.call-update) | async-done | bytes 65552 | tf_op jit(solution)/shard_map/reduce_scatter | solution.py:244
  254.4 26.0 %reduce-scatter.34.cloned.1.call-done = bf16[32,1,1024]{2,0,1:T(8,128)(2,1)} async-done(((bf16[128,1,1024]{2,0,1:T(8,128)(2,1)}), bf16[32,1,1024]{2,0,1:T(8,128)(2,1)}) %reduce-scatter.34.cloned.1.call-update) | async-done | bytes 65552 | tf_op jit(solution)/shard_map/reduce_scatter | solution.py:173
  282.1 9.3 %all_gather.49 = bf16[128,1,1024]{2,0,1:T(8,128)(2,1)S(1)} all-gather(bf16[32,1,1024]{2,0,1:T(8,128)(2,1)S(1)} %get-tuple-element.334), channel_id=1, replica_groups=mesh['dp'=2,'ctx'=4,'tp'=4] {'tp'}, dimensions={0}, use_global_device_ids=true | all-gather | bytes 327680 | tf_op jit(solution)/shard_map/all_gather | solution.py:261
  294.7 8.1 conditional.6
  313.6 11.3 %reduce-scatter.38.cloned.1.call-done = bf16[128,1,256]{2,0,1:T(8,128)(2,1)} async-done(((bf16[512,1,256]{2,0,1:T(8,128)(2,1)}), bf16[128,1,256]{2,0,1:T(8,128)(2,1)}) %reduce-scatter.38.cloned.1.call-update) | async-done | bytes 65552 | tf_op jit(solution)/shard_map/reduce_scatter | solution.py:329
  330.3 15.7 %reduce-scatter.58.cloned.1.call-done = bf16[128,256]{1,0:T(8,128)(2,1)} async-done(((bf16[512,256]{1,0:T(8,128)(2,1)}), bf16[128,256]{1,0:T(8,128)(2,1)}) %reduce-scatter.58.cloned.1.call-update) | async-done | bytes 65552 | tf_op jit(solution)/shard_map/reshape.177
  349.9 22.7 %reduce-scatter.40.cloned.1.call-done = bf16[32,1,1024]{2,0,1:T(8,128)(2,1)} async-done(((bf16[128,1,1024]{2,0,1:T(8,128)(2,1)}), bf16[32,1,1024]{2,0,1:T(8,128)(2,1)}) %reduce-scatter.40.cloned.1.call-update) | async-done | bytes 65552 | tf_op jit(solution)/shard_map/reduce_scatter | solution.py:356
  375.6 9.3 %all_gather.50 = bf16[128,1,1024]{2,0,1:T(8,128)(2,1)S(1)} all-gather(bf16[32,1,1024]{2,0,1:T(8,128)(2,1)S(1)} %fusion.272), channel_id=1, replica_groups=mesh['dp'=2,'ctx'=4,'tp'=4] {'tp'}, dimensions={0}, use_global_device_ids=true | all-gather | bytes 327680 | tf_op jit(solution)/shard_map/all_gather | solution.py:228
  392.1 22.4 %reduce-scatter.42.cloned.1.call-done = bf16[32,1,1024]{2,0,1:T(8,128)(2,1)} async-done(((bf16[128,1,1024]{2,0,1:T(8,128)(2,1)}), bf16[32,1,1024]{2,0,1:T(8,128)(2,1)}) %reduce-scatter.42.cloned.1.call-update) | async-done | bytes 65552 | tf_op jit(solution)/shard_map/reduce_scatter | solution.py:244
  417.8 9.5 %all_gather.51 = bf16[128,1,1024]{2,0,1:T(8,128)(2,1)S(1)} all-gather(bf16[32,1,1024]{2,0,1:T(8,128)(2,1)S(1)} %get-tuple-element.330), channel_id=1, replica_groups=mesh['dp'=2,'ctx'=4,'tp'=4] {'tp'}, dimensions={0}, use_global_device_ids=true | all-gather | bytes 327680 | tf_op jit(solution)/shard_map/all_gather | solution.py:261
  430.6 11.0 %conditional.7 = (f32[128,1,2,2,128]{4,0,3,2,1:T(8,128)}, bf16[512,1,256]{0,2,1:T(8,128)(2,1)}, bf16[512,1,256]{0,2,1:T(8,128)(2,1)}, f32[128,512]{1,0:T(8,128)S(1)}) conditional(s32[]{:T(128)} %convert_element_type.333, () %tuple.50, (s32[128]{0:T(128)S(1)}, bf16[512,1,256]{2,0,1:T(8,128)(2,1)S(1)}, bf16[128,1,2,2,128]{4,0,3,2,1:T(8,128)(2,1)}, ...), branch_computations={%region_34.35_spmd, %region_35.36_spmd} | conditional | flops 337773056 | bytes 10365500 | solution.py:326
  454.1 9.6 %reduce-scatter.44.cloned.1.call-done = bf16[128,1,256]{2,0,1:T(8,128)(2,1)} async-done(((bf16[512,1,256]{2,0,1:T(8,128)(2,1)}), bf16[128,1,256]{2,0,1:T(8,128)(2,1)}) %reduce-scatter.44.cloned.1.call-update) | async-done | bytes 65552 | tf_op jit(solution)/shard_map/reduce_scatter | solution.py:329
  466.9 18.0 %reduce-scatter.60.cloned.1.call-done = bf16[128,256]{1,0:T(8,128)(2,1)} async-done(((bf16[512,256]{1,0:T(8,128)(2,1)}), bf16[128,256]{1,0:T(8,128)(2,1)}) %reduce-scatter.60.cloned.1.call-update) | async-done | bytes 65552 | tf_op jit(solution)/shard_map/reshape.205
  530.6 39.0 %all-reduce = (f32[2,1024]{1,0:T(2,128)}, f32[2,128]{1,0:T(2,128)}, f32[2,128]{1,0:T(2,128)}, f32[2,1024]{1,0:T(2,128)}) all-reduce(f32[2,1024]{1,0:T(2,128)S(1)} %get-tuple-element.381, f32[2,128]{1,0:T(2,128)S(1)} %pad_maximum_fusion.16, ...), channel_id=1, replica_groups=mesh['dp'=2,'ctx'=4,'tp'=4] {'dp','ctx','tp'}, use_global_device_ids=true, to_apply=%region_44.45 | all-reduce | flops 4608 | bytes 36864 | tf_op jit(solution)/shard_map/psum | solution.py:409
  571.2 15.8 %reduce-scatter.52.cloned.1.call-done = bf16[2,128,256]{2,1,0:T(8,128)(2,1)} async-done(((bf16[2,1024,256]{2,1,0:T(8,128)(2,1)}), bf16[2,128,256]{2,1,0:T(8,128)(2,1)}) %reduce-scatter.52.cloned.1.call-update) | async-done | bytes 131088 | tf_op jit(solution)/shard_map/reduce_scatter | solution.py:392
  588.6 48.8 %reduce-scatter.62.cloned.1.call-done = bf16[128,1024]{1,0:T(8,128)(2,1)} async-done(((bf16[1024,1024]{1,0:T(8,128)(2,1)}), bf16[128,1024]{1,0:T(8,128)(2,1)}) %reduce-scatter.62.cloned.1.call-update) | async-done | bytes 262160
  639.6 48.2 %reduce-scatter.48.cloned.1.call-done = bf16[2,128,512]{2,1,0:T(8,128)(2,1)} async-done(((bf16[2,1024,512]{2,1,0:T(8,128)(2,1)}), bf16[2,128,512]{2,1,0:T(8,128)(2,1)}) %reduce-scatter.48.cloned.1.call-update) | async-done | bytes 262160 | tf_op jit(solution)/shard_map/reduce_scatter | solution.py:386
  689.6 68.0 %reduce-scatter.64.cloned.1.call-done = bf16[128,1536]{1,0:T(8,128)(2,1)} async-done(((bf16[1024,1536]{1,0:T(8,128)(2,1)}), bf16[128,1536]{1,0:T(8,128)(2,1)}) %reduce-scatter.64.cloned.1.call-update) | async-done | bytes 393232
  760.1 67.7 %reduce-scatter.54.cloned.1.call-done = bf16[2,128,768]{2,1,0:T(8,128)(2,1)} async-done(((bf16[2,1024,768]{2,1,0:T(8,128)(2,1)}), bf16[2,128,768]{2,1,0:T(8,128)(2,1)}) %reduce-scatter.54.cloned.1.call-update) | async-done | bytes 393232 | tf_op jit(solution)/shard_map/reduce_scatter | solution.py:398
  829.7 68.4 %reduce-scatter.56.cloned.1.call-done = bf16[2,128,768]{2,1,0:T(8,128)(2,1)} async-done(((bf16[2,1024,768]{2,1,0:T(8,128)(2,1)}), bf16[2,128,768]{2,1,0:T(8,128)(2,1)}) %reduce-scatter.56.cloned.1.call-update) | async-done | bytes 393232 | tf_op jit(solution)/shard_map/reduce_scatter | solution.py:401
  (564 shorter events, 206.7 us)
Async XLA Ops:
  7.2 81.3 %reduce-scatter.28.cloned.1.call-start = ((), (), s32[]{:S(2)}) async-start(), calls=%async_computation.19 | async-start | bytes 327680 | tf_op jit(solution)/shard_map/reduce_scatter | solution.py:145
  7.3 167.4 %copy-start.107 = (s32[128]{0:T(128)}, s32[128]{0:T(128)S(1)}, u32[]{:S(2)}) copy-start(s32[128]{0:T(128)S(1)} %iota_add_fusion) | copy-start | bytes 1540
  22.9 442.7 %copy-start.5 = (f32[128,256]{1,0:T(8,128)}, f32[128,256]{1,0:T(8,128)S(1)}, u32[]{:S(2)}) copy-start(f32[128,256]{1,0:T(8,128)S(1)} %fusion.172) | copy-start | bytes 393220
  23.1 121.3 %copy-start.124 = (f32[128]{0:T(128)}, f32[128]{0:T(128)S(1)}, u32[]{:S(2)}) copy-start(f32[128]{0:T(128)S(1)} %get-tuple-element.375) | copy-start | bytes 1540
  39.5 134.3 %copy-start.105 = (f32[128]{0:T(128)}, f32[128]{0:T(128)S(1)}, u32[]{:S(2)}) copy-start(f32[128]{0:T(128)S(1)} %get-tuple-element.373) | copy-start | bytes 1540
  65.0 64.2 %reduce-scatter.30.cloned.1.call-start = ((), (), s32[]{:S(2)}) async-start(), calls=%async_computation.20 | async-start | bytes 327680 | tf_op jit(solution)/shard_map/reduce_scatter | solution.py:173
  104.8 106.1 %reduce-scatter.32.cloned.1.call-start = ((), (), s32[]{:S(2)}) async-start(), calls=%async_computation.21 | async-start | bytes 327680 | tf_op jit(solution)/shard_map/reduce_scatter | solution.py:145
  140.7 186.9 %copy-start.7 = (f32[128,256]{1,0:T(8,128)}, f32[128,256]{1,0:T(8,128)S(1)}, u32[]{:S(2)}) copy-start(f32[128,256]{1,0:T(8,128)S(1)} %fusion.165) | copy-start | bytes 393220
  186.1 66.8 %reduce-scatter.36.cloned.1.call-start = ((), (), s32[]{:S(2)}) async-start(), calls=%async_computation.23 | async-start | bytes 327680 | tf_op jit(solution)/shard_map/reduce_scatter | solution.py:244
  228.3 52.1 %copy-start.86 = (f32[32,1,1024]{2,1,0:T(1,128)S(1)}, f32[32,1,1024]{2,1,0:T(1,128)}, u32[]{:S(2)}) copy-start(f32[32,1,1024]{2,1,0:T(1,128)} %param.33) | copy-start | bytes 393220
  228.4 52.1 %reduce-scatter.34.cloned.1.call-start = ((), (), s32[]{:S(2)}) async-start(), calls=%async_computation.22 | async-start | bytes 327680 | tf_op jit(solution)/shard_map/reduce_scatter | solution.py:173
  231.0 63.6 %copy-start.108 = (s32[128]{0:T(128)S(1)}, s32[128]{0:T(128)}, u32[]{:S(2)}) copy-start(s32[128]{0:T(128)} %copy-done.107) | copy-start | bytes 1540
  231.1 93.8 %reduce-scatter.38.cloned.1.call-start = ((), (), s32[]{:S(2)}) async-start(), calls=%async_computation.24 | async-start | bytes 327680 | tf_op jit(solution)/shard_map/reduce_scatter | solution.py:329
  304.7 41.3 %reduce-scatter.58.cloned.1.call-start = ((), (), s32[]{:S(2)}) async-start(), calls=%async_computation.34 | async-start | bytes 327680 | tf_op jit(solution)/shard_map/reshape.177
  311.0 61.6 %reduce-scatter.40.cloned.1.call-start = ((), (), s32[]{:S(2)}) async-start(), calls=%async_computation.25 | async-start | bytes 327680 | tf_op jit(solution)/shard_map/reduce_scatter | solution.py:356
  330.3 42.4 %copy-start.25 = (bf16[32,1,1024]{2,0,1:T(8,128)(2,1)S(1)}, bf16[32,1,1024]{2,0,1:T(8,128)(2,1)}, u32[]{:S(2)}) copy-start(bf16[32,1,1024]{2,0,1:T(8,128)(2,1)} %reduce-scatter.30.cloned.1.call-done) | copy-start | bytes 196612
  330.3 42.3 %copy-start.119 = (f32[32]{0:T(128)S(1)}, f32[32]{0:T(128)}, u32[]{:S(2)}) copy-start(f32[32]{0:T(128)} %copy-done.118) | copy-start | bytes 388
  330.3 44.4 %copy-start.49 = (f32[32,1,1024]{2,0,1:T(8,128)S(1)}, f32[32,1,1024]{2,0,1:T(8,128)}, u32[]{:S(2)}) copy-start(f32[32,1,1024]{2,0,1:T(8,128)} %get-tuple-element.335) | copy-start | bytes 393220
  349.9 64.6 %reduce-scatter.42.cloned.1.call-start = ((), (), s32[]{:S(2)}) async-start(), calls=%async_computation.26 | async-start | bytes 327680 | tf_op jit(solution)/shard_map/reduce_scatter | solution.py:244
  390.0 40.6 %copy-start.109 = (s32[128]{0:T(128)S(1)}, s32[128]{0:T(128)}, u32[]{:S(2)}) copy-start(s32[128]{0:T(128)} %copy-done.107) | copy-start | bytes 1540
  390.0 40.6 %copy-start.114 = (f32[1,2,2,128]{3,2,1,0:T(2,128)S(1)}, f32[1,2,2,128]{3,2,1,0:T(2,128)}, u32[]{:S(2)}) copy-start(f32[1,2,2,128]{3,2,1,0:T(2,128)} %copy-done.113) | copy-start | bytes 6148
  390.0 40.6 %copy-start.116 = (f32[1,2,2,128]{3,2,1,0:T(2,128)S(1)}, f32[1,2,2,128]{3,2,1,0:T(2,128)}, u32[]{:S(2)}) copy-start(f32[1,2,2,128]{3,2,1,0:T(2,128)} %copy-done.115) | copy-start | bytes 6148
  390.1 73.6 %reduce-scatter.44.cloned.1.call-start = ((), (), s32[]{:S(2)}) async-start(), calls=%async_computation.27 | async-start | bytes 327680 | tf_op jit(solution)/shard_map/reduce_scatter | solution.py:329
  443.5 41.3 %reduce-scatter.60.cloned.1.call-start = ((), (), s32[]{:S(2)}) async-start(), calls=%async_computation.35 | async-start | bytes 327680 | tf_op jit(solution)/shard_map/reshape.205
  451.5 76.2 %reduce-scatter.46.cloned.1.call-start = ((), (), s32[]{:S(2)}) async-start(), calls=%async_computation.28 | async-start | bytes 327680 | tf_op jit(solution)/shard_map/reduce_scatter | solution.py:356
  488.7 80.9 %reduce-scatter.50.cloned.1.call-start = ((), (), s32[]{:S(2)}) async-start(), calls=%async_computation.30 | async-start | bytes 1179648 | tf_op jit(solution)/shard_map/reduce_scatter | solution.py:389
  490.5 96.4 %reduce-scatter.52.cloned.1.call-start = ((), (), s32[]{:S(2)}) async-start(), calls=%async_computation.31 | async-start | bytes 1179648 | tf_op jit(solution)/shard_map/reduce_scatter | solution.py:392
  492.4 145.0 %reduce-scatter.62.cloned.1.call-start = ((), (), s32[]{:S(2)}) async-start(), calls=%async_computation.36 | async-start | bytes 2359296
  501.1 186.7 %reduce-scatter.48.cloned.1.call-start = ((), (), s32[]{:S(2)}) async-start(), calls=%async_computation.29 | async-start | bytes 2359296 | tf_op jit(solution)/shard_map/reduce_scatter | solution.py:386
  504.5 253.1 %reduce-scatter.64.cloned.1.call-start = ((), (), s32[]{:S(2)}) async-start(), calls=%async_computation.37 | async-start | bytes 3538944
  517.0 310.8 %reduce-scatter.54.cloned.1.call-start = ((), (), s32[]{:S(2)}) async-start(), calls=%async_computation.32 | async-start | bytes 3538944 | tf_op jit(solution)/shard_map/reduce_scatter | solution.py:398
  521.2 377.0 %reduce-scatter.56.cloned.1.call-start = ((), (), s32[]{:S(2)}) async-start(), calls=%async_computation.33 | async-start | bytes 3538944 | tf_op jit(solution)/shard_map/reduce_scatter | solution.py:401
  (126 other events, 1171.5 us)
Sparse Core Ops, SparseCore 0:
  65.2 23.2 reduce-scatter.27
  104.9 24.3 reduce-scatter.29
  186.2 24.6 reduce-scatter.31
  228.5 24.3 reduce-scatter.35
  256.1 24.3 reduce-scatter.33
  304.8 19.9 reduce-scatter.37
  327.7 18.2 reduce-scatter.57
  350.0 22.5 reduce-scatter.39
  390.2 24.2 reduce-scatter.41
  443.7 19.9 reduce-scatter.43
  466.5 18.2 reduce-scatter.59
  488.8 22.5 reduce-scatter.45
  513.6 35.9 reduce-scatter.49
  551.8 35.1 reduce-scatter.51
  589.1 48.1 reduce-scatter.61
  639.5 48.2 reduce-scatter.47
  689.9 67.6 reduce-scatter.63
  759.8 67.9 reduce-scatter.53
  830.1 67.9 reduce-scatter.55
where the time goes:
time: 918 us; the launch traced here: 907 us
  waiting for transfers between devices  525 us (57%)
  blocking collectives  171 us (19%)
  local copies, waits for them, and re-layouts  65.9 us (7%)
  matrix products  65.5 us (7%)
  other arithmetic  61.5 us (7%)
  between operations  16.6 us (2%)
    unnamed x21, waiting for transfers between devices  117 us
    reduce_scatter x1, waiting for transfers between devices, on_device(): lax.psum_scatter(stacked[5].astype(jnp.bfloat16), ('dp', 'ctx'), scatter_...  68.4 us
    reduce_scatter x1, waiting for transfers between devices, on_device(): lax.psum_scatter(stacked[4].astype(jnp.bfloat16), ('dp', 'ctx'), scatter_...  67.7 us
    reduce_scatter x2, waiting for transfers between devices, on_device(): lax.psum_scatter(jnp.einsum('rsf,fd->rsd', forward_swish, down_weight[ind...  50.4 us
    reduce_scatter x1, waiting for transfers between devices, on_device(): lax.psum_scatter(stacked[0].astype(jnp.bfloat16), ('dp', 'ctx'), scatter_...  48.2 us
    reduce_scatter x2, waiting for transfers between devices, on_device(): lax.psum_scatter((jnp.einsum('rsf,df->rsd', grad_gate, gate_weight[index]...  42.8 us
    psum x1, blocking collectives, on_device(): lax.psum((gains[0], gains[1], gains[2], gains[3]), ('dp', 'ctx', 'tp'))  39 us
    unnamed x277, local copies, waits for them, and re-layouts  37.2 us
  transfers between devices with their start and end apart: 19, of which 17 were waited for; matrix products, arithmetic and copies ran while one was open for 9% of the time, Pallas kernels for 0%

commit v1 on v0

v1 whole, which is shorter than its diff:
```python
import functools

import jax
import jax.numpy as jnp
from jax import lax
from jax.experimental import pallas as pl
from jax.experimental.pallas import tpu as pltpu
from jax.sharding import PartitionSpec as P

EPS = 1e-06
THETA = 1000000.0
MESH = pl.DeviceIdType.MESH
F32 = jnp.float32
BF16 = jnp.bfloat16


def rms_forward(field, gain):
    inverse = lax.rsqrt(jnp.mean(field * field, axis=-1, keepdims=True) + EPS)
    normed = field * inverse
    return (normed * gain, normed, inverse)


def rms_backward(grad_out, normed, inverse, gain):
    scaled = grad_out * gain
    return inverse * (scaled - normed * jnp.mean(scaled * normed, axis=-1, keepdims=True))


def rope_tables(positions, head_dim):
    half = head_dim // 2
    frequency = THETA ** (-(2.0 * jnp.arange(half, dtype=F32)) / head_dim)
    angles = positions[:, None] * frequency[None, :]
    angles = jnp.concatenate([angles, angles], axis=-1)
    return (jnp.cos(angles)[:, None, :], jnp.sin(angles)[:, None, :])


def rotate(field, cosine, sine):
    half = field.shape[-1] // 2
    turned = jnp.concatenate([-field[..., half:], field[..., :half]], axis=-1)
    return field * cosine + turned * sine


def remote(src, dst, send, recv, **where):
    return pltpu.make_async_remote_copy(
        src_ref=src,
        dst_ref=dst,
        send_sem=send,
        recv_sem=recv,
        device_id=where,
        device_id_type=MESH,
    )


def boundary_kernel(mode, n_ctx, n_tp, *refs):
    refs = list(refs)
    has_sum = mode != "first"
    has_gather = mode in ("first", "fwd", "bwd")
    partial = refs.pop(0) if has_sum else None
    stream = refs.pop(0)
    gain = refs.pop(0) if mode not in ("fwd_last",) else None
    grad_res = refs.pop(0) if mode in ("bwd", "bwd_last") else None
    fresh = refs.pop(0) if mode != "first" else None
    gain_part = refs.pop(0) if mode in ("bwd", "bwd_last") else None
    out = refs.pop(0) if has_gather else None
    if has_sum:
        landed, rs_send, rs_recv = refs.pop(0), refs.pop(0), refs.pop(0)
    if has_gather:
        own, z_send, z_recv, t_send, t_recv = refs

    me_c = lax.axis_index("ctx")
    me_t = lax.axis_index("tp")
    tp_peers = [lax.rem(me_t + d, n_tp) for d in range(1, n_tp)]
    ctx_peers = [lax.rem(me_c + d, n_ctx) for d in range(1, n_ctx)] if has_gather else []
    barrier = pltpu.get_barrier_semaphore()
    for peer in tp_peers:
        pl.semaphore_signal(barrier, inc=1, device_id={"tp": peer}, device_id_type=MESH)
    for peer in ctx_peers:
        pl.semaphore_signal(barrier, inc=1, device_id={"ctx": peer}, device_id_type=MESH)
    pl.semaphore_wait(barrier, len(tp_peers) + len(ctx_peers))

    if has_sum:
        sums = [
            remote(partial.at[peer], landed.at[d], rs_send.at[d], rs_recv.at[d], tp=peer)
            for d, peer in enumerate(tp_peers)
        ]
        for copy in sums:
            copy.start()
        total = partial[me_t].astype(F32)
        for d, copy in enumerate(sums):
            copy.wait_recv()
            total = total + landed[d].astype(F32)
        for copy in sums:
            copy.wait_send()

    field = stream[...]
    if mode == "first":
        sent = rms_forward(field, gain[...])[0].astype(BF16)
    elif mode in ("fwd", "fwd_last"):
        field = field + total
        fresh[...] = field
        if mode == "fwd":
            sent = rms_forward(field, gain[...])[0].astype(BF16)
    else:
        _, normed, inverse = rms_forward(field, gain[...])
        gain_part[...] = jnp.sum(total * normed, axis=0, keepdims=True)
        field = grad_res[...] + rms_backward(total, normed, inverse, gain[...])
        fresh[...] = field
        sent = field.astype(BF16)

    if has_gather:
        own[...] = sent
        copies = []
        for d, peer in enumerate(ctx_peers):
            copies.append(
                remote(own, out.at[me_c, me_t], z_send.at[d], z_recv.at[d], ctx=peer)
            )
        for d, peer in enumerate(tp_peers):
            copies.append(
                remote(own, out.at[me_c, me_t], t_send.at[0, d], t_recv.at[0, d], tp=peer)
            )
        for copy in copies:
            copy.start()
        out[me_c, me_t] = sent
        for d in range(n_ctx - 1):
            source = lax.rem(me_c + n_ctx - (d + 1), n_ctx)
            slot = out.at[source, me_t]
            remote(own, slot, z_send.at[d], z_recv.at[d], ctx=source).wait_recv()
            for k, peer in enumerate(tp_peers):
                copy = remote(slot, slot, t_send.at[d + 1, k], t_recv.at[d + 1, k], tp=peer)
                copy.start()
                copies.append(copy)
        for d in range(n_ctx):
            source = lax.rem(me_c + n_ctx - d, n_ctx)
            for k in range(n_tp - 1):
                origin = lax.rem(me_t + n_tp - (k + 1), n_tp)
                remote(
                    own, out.at[source, origin], t_send.at[d, k], t_recv.at[d, k], tp=origin
                ).wait_recv()
        for copy in copies:
            copy.wait_send()


IDS = {"first": 0, "fwd": 1, "fwd_last": 2, "bwd": 3, "bwd_last": 4}


def boundary(mode, stream, gain=None, partial=None, grad_res=None):
    n_ctx, n_tp = lax.axis_size("ctx"), lax.axis_size("tp")
    rows, width = stream.shape
    operands = []
    if partial is not None:
        operands.append(partial.reshape(n_tp, rows, width))
    operands.append(stream)
    if gain is not None:
        operands.append(gain.reshape(1, width))
    if grad_res is not None:
        operands.append(grad_res)
    shapes = []
    if mode != "first":
        shapes.append(jax.ShapeDtypeStruct((rows, width), F32))
    if grad_res is not None:
        shapes.append(jax.ShapeDtypeStruct((1, width), F32))
    scratch = []
    dma = pltpu.SemaphoreType.DMA
    if partial is not None:
        scratch += [pltpu.VMEM((n_tp - 1, rows, width), BF16), dma((n_tp - 1,)), dma((n_tp - 1,))]
    if mode in ("first", "fwd", "bwd"):
        shapes.append(jax.ShapeDtypeStruct((n_ctx, n_tp, rows, width), BF16))
        scratch += [
            pltpu.VMEM((rows, width), BF16),
            dma((n_ctx - 1,)),
            dma((n_ctx - 1,)),
            dma((n_ctx, n_tp - 1)),
            dma((n_ctx, n_tp - 1)),
        ]
    vmem = pl.BlockSpec(memory_space=pltpu.VMEM)
    outs = pl.pallas_call(
        functools.partial(boundary_kernel, mode, n_ctx, n_tp),
        out_shape=shapes,
        in_specs=[vmem] * len(operands),
        out_specs=[vmem] * len(shapes),
        scratch_shapes=scratch,
        name="boundary_" + mode,
        compiler_params=pltpu.CompilerParams(
            collective_id=IDS[mode], has_side_effects=True, vmem_limit_bytes=32 * 2**20
        ),
    )(*operands)
    outs = list(outs)
    if mode in ("first", "fwd", "bwd"):
        outs[-1] = outs[-1].reshape(n_ctx * n_tp * rows, width)
    return outs


def gains_kernel(sizes, x_ref, o_ref, cur, land_0, land_1, land_2, send, recv):
    lands = (land_0, land_1, land_2)
    axes = list(sizes)
    barrier = pltpu.get_barrier_semaphore()
    peers = {}
    count = 0
    for axis in axes:
        me = lax.axis_index(axis)
        peers[axis] = [lax.rem(me + d, sizes[axis]) for d in range(1, sizes[axis])]
        for peer in peers[axis]:
            pl.semaphore_signal(barrier, inc=1, device_id={axis: peer}, device_id_type=MESH)
            count += 1
    pl.semaphore_wait(barrier, count)
    total = x_ref[...]
    base = 0
    for step, axis in enumerate(axes):
        cur[step] = total
        copies = [
            remote(
                cur.at[step], lands[step].at[d], send.at[base + d], recv.at[base + d], **{axis: peer}
            )
            for d, peer in enumerate(peers[axis])
        ]
        for copy in copies:
            copy.start()
        me = lax.axis_index(axis)
        parts = []
        for d, copy in enumerate(copies):
            copy.wait_recv()
        acc = jnp.zeros_like(total)
        for position in range(sizes[axis]):
            offset = lax.rem(me + sizes[axis] - position, sizes[axis])
            slot = jnp.maximum(offset - 1, 0)
            acc = acc + jnp.where(offset == 0, total, lands[step][slot])
        total = acc
        for copy in copies:
            copy.wait_send()
        base += len(copies)
    o_ref[...] = total


def sum_gains(x):
    sizes = {axis: lax.axis_size(axis) for axis in ("dp", "ctx", "tp")}
    count = sum(n - 1 for n in sizes.values())
    vmem = pl.BlockSpec(memory_space=pltpu.VMEM)
    return pl.pallas_call(
        functools.partial(gains_kernel, sizes),
        out_shape=jax.ShapeDtypeStruct(x.shape, F32),
        in_specs=[vmem],
        out_specs=vmem,
        scratch_shapes=[pltpu.VMEM((3,) + x.shape, F32)]
        + [pltpu.VMEM((max(n - 1, 1),) + x.shape, F32) for n in sizes.values()]
        + [pltpu.SemaphoreType.DMA((count,)), pltpu.SemaphoreType.DMA((count,))],
        name="sum_gains",
        compiler_params=pltpu.CompilerParams(collective_id=5, has_side_effects=True),
    )(x)


NT = (((1,), (1,)), ((), ()))
NN = (((1,), (0,)), ((), ()))
TN = (((0,), (0,)), ((), ()))


def dot(a, b, dims):
    return lax.dot_general(a, b, dims, preferred_element_type=F32)


def soft_weights(scale, bq, q, k):
    rows = pl.program_id(2) * bq + lax.broadcasted_iota(jnp.int32, (bq, k.shape[0]), 0)
    cols = lax.broadcasted_iota(jnp.int32, (bq, k.shape[0]), 1)
    scores = jnp.where(cols <= rows, dot(q, k, NT) * scale, -jnp.inf)
    weights = jnp.exp(scores - jnp.max(scores, axis=-1, keepdims=True))
    return weights, jnp.sum(weights, axis=-1, keepdims=True)


def attend_kernel(scale, bq, q_ref, k_ref, v_ref, o_ref):
    weights, total = soft_weights(scale, bq, q_ref[...], k_ref[...])
    o_ref[...] = (dot(weights.astype(BF16), v_ref[...], NN) / total).astype(BF16)


def attend_back_kernel(scale, bq, q_ref, k_ref, v_ref, o_ref, do_ref, dq_ref, dk_ref, dv_ref):
    q, k, do = q_ref[...], k_ref[...], do_ref[...]
    weights, total = soft_weights(scale, bq, q, k)
    probs = weights / total
    delta = jnp.sum(do.astype(F32) * o_ref[...].astype(F32), axis=-1, keepdims=True)
    dscore = (probs * (dot(do, v_ref[...], NT) - delta)).astype(BF16)
    dq_ref[...] = dot(dscore, k, NN) * scale

    @pl.when((pl.program_id(1) == 0) & (pl.program_id(2) == 0))
    def _():
        dk_ref[...] = jnp.zeros_like(dk_ref)
        dv_ref[...] = jnp.zeros_like(dv_ref)

    dk_ref[...] += dot(dscore, q, TN) * scale
    dv_ref[...] += dot(probs.astype(BF16), do, TN)


def attention(back, scale, group, head_dim, *operands):
    length, kv_width = operands[1].shape
    kv_heads = kv_width // head_dim
    bq = min(length, 256)
    rows = pl.BlockSpec((bq, head_dim), lambda h, g, i: (i, h * group + g))
    keys = pl.BlockSpec((length, head_dim), lambda h, g, i: (0, h))
    wide = jax.ShapeDtypeStruct((length, kv_width * group), F32 if back else BF16)
    narrow = jax.ShapeDtypeStruct((length, kv_width), F32)
    work = 2 * length * length * head_dim * kv_heads * group
    return pl.pallas_call(
        functools.partial(attend_back_kernel if back else attend_kernel, scale, bq),
        grid=(kv_heads, group, length // bq),
        out_shape=(wide, narrow, narrow) if back else wide,
        in_specs=[rows, keys, keys] + ([rows, rows] if back else []),
        out_specs=(rows, keys, keys) if back else rows,
        name="attend_back" if back else "attend",
        cost_estimate=pl.CostEstimate(
            flops=work * (5 if back else 2), bytes_accessed=4 * length * 1024, transcendentals=0
        ),
        compiler_params=pltpu.CompilerParams(vmem_limit_bytes=32 * 2**20),
    )(*operands)


def on_device(
    block_input,
    input_gain,
    query_weight,
    key_weight,
    value_weight,
    query_gain,
    key_gain,
    out_weight,
    post_gain,
    gate_weight,
    up_weight,
    down_weight,
    grad_output,
):
    local_rows, seq_local, width = block_input.shape
    assert seq_local == 1 and lax.axis_size("dp") == 2
    layers = input_gain.shape[0]
    head_dim = query_gain.shape[-1]
    heads = query_weight.shape[-1] // head_dim
    kv_heads = key_weight.shape[-1] // head_dim
    n_ctx, n_tp = lax.axis_size("ctx"), lax.axis_size("tp")
    block_rows = local_rows * n_tp
    length = block_rows * n_ctx
    scale = head_dim ** (-0.5)
    first_row = lax.axis_index("ctx") * block_rows
    cosine, sine = rope_tables(jnp.arange(length, dtype=F32), head_dim)
    piece = width // (2 * n_ctx)
    my_cols = (lax.axis_index("dp") * n_ctx + lax.axis_index("ctx")) * piece
    other_cols = ((1 - lax.axis_index("dp")) * n_ctx + lax.axis_index("ctx")) * piece
    swap = [(0, 1), (1, 0)]

    def mine(x):
        return lax.dynamic_slice_in_dim(x, first_row, block_rows, 0)

    def slices(x):
        parts = [lax.dynamic_slice_in_dim(x, at, piece, 1) for at in (my_cols, other_cols)]
        return jnp.concatenate(parts, axis=1)

    def settle(grad, axis):
        own, other = jnp.split(grad, 2, axis=axis)
        return own + lax.ppermute(other.astype(BF16), "dp", swap).astype(F32)

    def heads_of(x, count):
        return x.reshape(length, count, head_dim)

    attend_args = (scale, heads // kv_heads, head_dim)
    hidden = block_input[:, 0]
    grad_hidden = grad_output[:, 0]
    grad_rows = lax.all_gather(grad_hidden.astype(BF16), ("ctx", "tp"), axis=0, tiled=True)
    (first_in,) = boundary("first", hidden, input_gain[0])
    kept = []
    for l in range(layers):
        query = dot(first_in, query_weight[l], NN)
        keys = dot(first_in, key_weight[l], NN)
        values = dot(first_in, value_weight[l], NN).astype(BF16)
        query_normed, q_plain, q_inv = rms_forward(heads_of(query, heads), query_gain[l])
        key_normed, k_plain, k_inv = rms_forward(heads_of(keys, kv_heads), key_gain[l])
        query_rot = rotate(query_normed, cosine, sine).astype(BF16).reshape(length, -1)
        key_rot = rotate(key_normed, cosine, sine).astype(BF16).reshape(length, -1)
        attended = attention(False, *attend_args, query_rot, key_rot, values)
        partial = dot(mine(attended), out_weight[l], NN).astype(BF16)
        mixed, second_in = boundary("fwd", hidden, post_gain[l], partial)
        gate = dot(second_in, gate_weight[l], NN)
        upward = dot(second_in, up_weight[l], NN)
        swish = (jax.nn.silu(gate) * upward).astype(BF16)
        partial = dot(mine(swish), down_weight[l], NN).astype(BF16)
        kept.append(
            (hidden, first_in, q_plain, q_inv, k_plain, k_inv, query_rot, key_rot, values)
            + (attended, mixed, second_in, gate, upward, swish)
        )
        if l + 1 < layers:
            hidden, first_in = boundary("fwd", mixed, input_gain[l + 1], partial)
        else:
            (hidden,) = boundary("fwd_last", mixed, None, partial)

    grads = [None] * layers
    gains = [None] * layers
    for l in reversed(range(layers)):
        (x_in, first_in, q_plain, q_inv, k_plain, k_inv, query_rot, key_rot, values) = kept[l][:9]
        attended, mixed, second_in, gate, upward, swish = kept[l][9:]
        grad_swish = dot(grad_rows, down_weight[l], NT)
        sigma = jax.nn.sigmoid(gate)
        grad_gate = (grad_swish * upward * (sigma * (1.0 + gate * (1.0 - sigma)))).astype(BF16)
        grad_up = (grad_swish * (gate * sigma)).astype(BF16)
        partial = dot(mine(grad_gate), gate_weight[l], NT) + dot(mine(grad_up), up_weight[l], NT)
        grad_mixed, post_part, mixed_rows = boundary(
            "bwd", mixed, post_gain[l], partial.astype(BF16), grad_hidden
        )
        second_cols = slices(second_in)
        down_grad = settle(dot(swish, slices(grad_rows), TN), 1)
        gate_grad = settle(dot(second_cols, grad_gate, TN), 0)
        up_grad = settle(dot(second_cols, grad_up, TN), 0)

        grad_heads = dot(mixed_rows, out_weight[l], NT).astype(BF16)
        out_grad = settle(dot(attended, slices(mixed_rows), TN), 1)
        grad_query, grad_keys, grad_values = attention(
            True, *attend_args, query_rot, key_rot, values, attended, grad_heads
        )
        grad_query = rotate(heads_of(grad_query, heads), cosine, -sine)
        grad_keys = rotate(heads_of(grad_keys, kv_heads), cosine, -sine)
        q_part = jnp.sum(mine(grad_query * q_plain), axis=(0, 1))
        k_part = jnp.sum(mine(grad_keys * k_plain), axis=(0, 1))
        query_bf = rms_backward(grad_query, q_plain, q_inv, query_gain[l]).astype(BF16)
        key_bf = rms_backward(grad_keys, k_plain, k_inv, key_gain[l]).astype(BF16)
        query_bf = query_bf.reshape(length, -1)
        key_bf = key_bf.reshape(length, -1)
        value_bf = grad_values.astype(BF16)
        partial = (
            dot(mine(query_bf), query_weight[l], NT)
            + dot(mine(key_bf), key_weight[l], NT)
            + dot(mine(value_bf), value_weight[l], NT)
        ).astype(BF16)
        if l:
            grad_hidden, input_part, grad_rows = boundary(
                "bwd", x_in, input_gain[l], partial, grad_mixed
            )
        else:
            grad_hidden, input_part = boundary(
                "bwd_last", x_in, input_gain[l], partial, grad_mixed
            )
        first_cols = slices(first_in)
        query_grad = settle(dot(first_cols, query_bf, TN), 0)
        key_grad = settle(dot(first_cols, key_bf, TN), 0)
        value_grad = settle(dot(first_cols, value_bf, TN), 0)
        grads[l] = (query_grad, key_grad, value_grad, out_grad, gate_grad, up_grad, down_grad)
        gains[l] = (input_part[0], q_part, k_part, post_part[0])
    stacked = [jnp.stack([part[m] for part in grads]) for m in range(7)]
    packed = jnp.concatenate([v for part in gains for v in part])
    sizes = [v.shape[0] for part in gains for v in part]
    padded = -(-packed.shape[0] // 1024) * 1024
    packed = jnp.pad(packed, (0, padded - packed.shape[0])).reshape(-1, 128)
    summed = sum_gains(packed).reshape(-1)
    pieces = []
    at = 0
    for size in sizes:
        pieces.append(summed[at : at + size])
        at += size
    gains = [jnp.stack([pieces[4 * l + m] for l in range(layers)]) for m in range(4)]
    return (
        hidden[:, None],
        grad_hidden[:, None],
        gains[0],
        stacked[0],
        stacked[1],
        stacked[2],
        gains[1],
        gains[2],
        stacked[3],
        gains[3],
        stacked[4],
        stacked[5],
        stacked[6],
    )


def solution(mesh):
    placed = (
        P(("ctx", "tp"), "dp", None),
        P(),
        P(None, None, "tp"),
        P(None, None, "tp"),
        P(None, None, "tp"),
        P(),
        P(),
        P(None, "tp", None),
        P(),
        P(None, None, "tp"),
        P(None, None, "tp"),
        P(None, "tp", None),
        P(("ctx", "tp"), "dp", None),
    )
    return jax.shard_map(
        on_device,
        mesh=mesh,
        in_specs=placed,
        out_specs=(
            P(("ctx", "tp"), "dp", None),
            P(("ctx", "tp"), "dp", None),
            P(),
            P(None, ("dp", "ctx"), "tp"),
            P(None, ("dp", "ctx"), "tp"),
            P(None, ("dp", "ctx"), "tp"),
            P(),
            P(),
            P(None, "tp", ("dp", "ctx")),
            P(),
            P(None, ("dp", "ctx"), "tp"),
            P(None, ("dp", "ctx"), "tp"),
            P(None, "tp", ("dp", "ctx")),
        ),
        check_vma=False,
    )
```

time: 918 us -> 331 us (0.36); the launches traced: 907 us -> 330 us
  waiting for transfers between devices: 525 us -> 6.18 us
  Pallas kernels: 0 us -> 185 us
  blocking collectives: 171 us -> 0 us
  other arithmetic: 61.5 us -> 27.1 us
  local copies, waits for them, and re-layouts: 65.9 us -> 43.9 us
  matrix products: 65.5 us -> 48 us
    reduce_scatter x15 -> x0, waiting for transfers between devices: 374 us -> none  [the longest x1 68.4 us: on_device(): lax.psum_scatter(stacked[5].astype(jnp.bfloat16), ('dp', 'ctx'), scatter_...]
    pallas_call x0 -> x14, Pallas kernels: none -> 185 us  [the longest x9 148 us: boundary(): pl.pallas_call(functools.partial(boundary_kernel, mode, n_ctx, n_tp), out...]
    all_gather x12 -> x0, blocking collectives: 133 us -> none  [the longest x2 29 us: on_device(): lax.all_gather(forward_key_rot, 'ctx', axis=0, tiled=True)]
    unnamed x21 -> x1, waiting for transfers between devices: 117 us -> 0.02 us
    psum x1 -> x0, blocking collectives: 39 us -> none  [on_device(): lax.psum((gains[0], gains[1], gains[2], gains[3]), ('dp', 'ctx', 'tp'))]
    another operation x2 -> x0, waiting for transfers between devices: 33.6 us -> none
    convert_element_type x25 -> x10, other arithmetic: 25.5 us -> 3.28 us  [the longest x2 1.45 us: on_device(): rotate(query_normed, cosine, sine).astype(BF16).reshape(length, -1)]
    unnamed x277 -> x236, local copies, waits for them, and re-layouts: 37.2 us -> 17.5 us
  transfers between devices with their start and end apart: 19 -> 15, of which waited for: 17 -> 6; matrix products, arithmetic and copies ran while one was open for 9% -> 16% of each run, Pallas kernels for 0% -> 27%
where the time goes in v1:
time: 331 us; the launch traced here: 330 us
  Pallas kernels  185 us (56%)
  matrix products  48 us (15%)
  local copies, waits for them, and re-layouts  43.9 us (13%)
  other arithmetic  27.1 us (8%)
  between operations  15.9 us (5%)
  waiting for transfers between devices  6.18 us (2%)
  starting transfers between devices  3.79 us (1%)
    pallas_call x9, Pallas kernels, boundary(): pl.pallas_call(functools.partial(boundary_kernel, mode, n_ctx, n_tp), out...  148 us
    dot_general x42, matrix products, dot(): return lax.dot_general(a, b, dims, preferred_element_type=F32)  48 us
    pallas_call x4, Pallas kernels, attention(): pl.pallas_call(functools.partial(attend_back_kernel if back else attend_k...  25.9 us
    unnamed x236, local copies, waits for them, and re-layouts  17.5 us
    pallas_call x1, Pallas kernels, sum_gains(): pl.pallas_call(functools.partial(gains_kernel, sizes), out_shape=jax.Shap...  11.8 us
    dot_general x6, local copies, waits for them, and re-layouts, dot(): return lax.dot_general(a, b, dims, preferred_element_type=F32)  8.52 us
  transfers between devices with their start and end apart: 15, of which 6 were waited for; matrix products, arithmetic and copies ran while one was open for 16% of the time, Pallas kernels for 27%

profile of v1, /device:TPU:0, one launch (start us, length us, event | category | flops | bytes accessed | tf_op | source)
XLA Modules:
  0.0 330.2 jit_solution(15744023257622665720)
XLA Ops:
  7.2 1.6 copy.64
  15.0 1.6 fusion.174
  18.7 19.4 %boundary_first.1 = bf16[4,4,32,1024]{3,2,1,0:T(8,128)(2,1)S(1)} custom-call(f32[32,1024]{1,0:T(8,128)S(1)} %bitcast.220, f32[1,1024]{1,0:T(1,128)S(1)} %get-tuple-element.143.refs_1_.refs_2_), custom_call_target="tpu_custom_call" | custom-call | tf_op jit(solution)/shard_map/boundary_first/pallas_call | solution.py:175
  40.9 2.8 slice_bitcast_fusion
  43.8 2.3 copy.30
  47.4 2.0 multiply_reduce_fusion.3
  53.1 1.6 convolution_convert_fusion.5.v_ref
  54.8 4.2 %attend.2.o_ref = bf16[512,512]{1,0:T(8,128)(2,1)S(1)} custom-call(bf16[512,512]{1,0:T(8,128)(2,1)S(1)} %copy.48.q_ref, bf16[512,256]{1,0:T(8,128)(2,1)S(1)} %copy.49.k_ref, bf16[512,256]{1,0:T(8,128)(2,1)S(1)} %convolution_convert_fusion.5.v_ref), custom_call_target="tpu_custom_call" | custom-call | flops 536870912 | bytes 2097152 | tf_op jit(solution)/shard_map/attend/pallas_call | solution.py:298
  60.1 20.5 %boundary_fwd.3 = (f32[32,1024]{1,0:T(8,128)S(1)}, bf16[4,4,32,1024]{3,2,1,0:T(8,128)(2,1)S(1)}) custom-call(bf16[4,32,1024]{2,1,0:T(8,128)(2,1)S(1)} %bitcast.235, f32[32,1024]{1,0:T(8,128)S(1)} %bitcast.221, f32[1,1024]{1,0:T(1,128)S(1)} %get-tuple-element.141.refs_2_), custom_call_target="tpu_custom_call" | custom-call | tf_op jit(solution)/shard_map/boundary_fwd/pallas_call | solution.py:175
  82.9 2.2 multiply_convert_fusion.5
  86.3 19.4 %boundary_fwd.4 = (f32[32,1024]{1,0:T(8,128)S(1)}, bf16[4,4,32,1024]{3,2,1,0:T(8,128)(2,1)S(1)}) custom-call(bf16[4,32,1024]{2,1,0:T(8,128)(2,1)S(1)} %bitcast.233, f32[32,1024]{1,0:T(8,128)S(1)} %get-tuple-element.37.refs_1_, f32[1,1024]{1,0:T(1,128)S(1)} %get-tuple-element.142.refs_2_), custom_call_target="tpu_custom_call" | custom-call | tf_op jit(solution)/shard_map/boundary_fwd/pallas_call | solution.py:175
  106.2 1.8 multiply_reduce_fusion.2
  109.6 2.3 broadcast_multiply_fusion
  113.5 1.9 convolution_convert_fusion.3.v_ref
  115.5 4.4 %attend.3.o_ref = bf16[512,512]{1,0:T(8,128)(2,1)S(1)} custom-call(bf16[512,512]{1,0:T(8,128)(2,1)S(1)} %copy.50.q_ref, bf16[512,256]{1,0:T(8,128)(2,1)S(1)} %copy.51.k_ref, bf16[512,256]{1,0:T(8,128)(2,1)S(1)} %convolution_convert_fusion.3.v_ref), custom_call_target="tpu_custom_call" | custom-call | flops 536870912 | bytes 2097152 | tf_op jit(solution)/shard_map/attend/pallas_call | solution.py:298
  120.2 20.6 %boundary_fwd.5 = (f32[32,1024]{1,0:T(8,128)S(1)}, bf16[4,4,32,1024]{3,2,1,0:T(8,128)(2,1)S(1)}) custom-call(bf16[4,32,1024]{2,1,0:T(8,128)(2,1)S(1)} %bitcast.234, f32[32,1024]{1,0:T(8,128)S(1)} %get-tuple-element.39.refs_1_, f32[1,1024]{1,0:T(1,128)S(1)} %get-tuple-element.140.refs_2_), custom_call_target="tpu_custom_call" | custom-call | tf_op jit(solution)/shard_map/boundary_fwd/pallas_call | solution.py:175
  142.0 2.2 fusion.6
  144.2 2.9 fusion
  147.2 4.0 %multiply_convert_fusion.3 = (bf16[512,768]{1,0:T(8,128)(2,1)S(1)}, bf16[512,768]{1,0:T(8,128)(2,1)S(1)}, bf16[512,768]{1,0:T(8,128)(2,1)}) fusion(f32[512,768]{1,0:T(8,128)S(1)} %fusion, f32[512,768]{1,0:T(8,128)} %fusion.6, bf16[512,1024]{1,0:T(8,128)(2,1)S(1)} %bitcast.253, bf16[2,1024,768]{2,1,0:T(8,128)(2,1)S(1)} %copy-done.51), kind=kOutput, calls=%fused_computation.27 | convolution fusion | flops 811204608 | bytes 8126464 | tf_op jit(solution)/shard_map/dot_general | solution.py:256
  155.1 19.5 %boundary_bwd.3 = (f32[32,1024]{1,0:T(8,128)S(1)}, f32[1,1024]{1,0:T(1,128)S(1)}, bf16[4,4,32,1024]{3,2,1,0:T(8,128)(2,1)S(1)}) custom-call(bf16[4,32,1024]{2,1,0:T(8,128)(2,1)S(1)} %bitcast.227, f32[32,1024]{1,0:T(8,128)S(1)} %get-tuple-element.41.refs_1_, f32[1,1024]{1,0:T(1,128)S(1)} %get-tuple-element.140.refs_2_, f32[32,1024]{1,0:T(8,128)S(1)} %bitcast.231), custom_call_target="tpu_custom_call" | custom-call | tf_op jit(solution)/shard_map/boundary_bwd/pallas_call | solution.py:175
  175.9 1.8 constant_dynamic-slice_fusion.7
  178.9 8.6 %attend_back.2 = (f32[512,512]{1,0:T(8,128)S(1)}, f32[512,256]{1,0:T(8,128)S(1)}, f32[512,256]{1,0:T(8,128)S(1)}) custom-call(bf16[512,512]{1,0:T(8,128)(2,1)S(1)} %copy.50.q_ref, bf16[512,256]{1,0:T(8,128)(2,1)S(1)} %copy-done.5, bf16[512,256]{1,0:T(8,128)(2,1)S(1)} %copy-done.23, bf16[512,512]{1,0:T(8,128)(2,1)S(1)} %copy-done.18, ...), custom_call_target="tpu_custom_call" | custom-call | flops 1342177280 | bytes 2097152 | tf_op jit(solution)/shard_map/attend_back/pallas_call | solution.py:298
  195.1 1.8 copy-done.33
  197.4 18.5 %boundary_bwd.4 = (f32[32,1024]{1,0:T(8,128)S(1)}, f32[1,1024]{1,0:T(1,128)S(1)}, bf16[4,4,32,1024]{3,2,1,0:T(8,128)(2,1)S(1)}) custom-call(bf16[4,32,1024]{2,1,0:T(8,128)(2,1)S(1)} %bitcast.228, f32[32,1024]{1,0:T(8,128)S(1)} %get-tuple-element.39.refs_1_, f32[1,1024]{1,0:T(1,128)S(1)} %get-tuple-element.142.refs_2_, f32[32,1024]{1,0:T(8,128)S(1)} %copy-done.7), custom_call_target="tpu_custom_call" | custom-call | tf_op jit(solution)/shard_map/boundary_bwd/pallas_call | solution.py:175
  222.0 18.4 %boundary_bwd.5 = (f32[32,1024]{1,0:T(8,128)S(1)}, f32[1,1024]{1,0:T(1,128)S(1)}, bf16[4,4,32,1024]{3,2,1,0:T(8,128)(2,1)S(1)}) custom-call(bf16[4,32,1024]{2,1,0:T(8,128)(2,1)S(1)} %bitcast.229, f32[32,1024]{1,0:T(8,128)S(1)} %get-tuple-element.37.refs_1_, f32[1,1024]{1,0:T(1,128)S(1)} %get-tuple-element.141.refs_2_, f32[32,1024]{1,0:T(8,128)S(1)} %get-tuple-element.48.refs_3_), custom_call_target="tpu_custom_call" | custom-call | tf_op jit(solution)/shard_map/boundary_bwd/pallas_call | solution.py:175
  240.5 1.8 constant_dynamic-slice_fusion.11
  246.1 8.7 %attend_back.3 = (f32[512,512]{1,0:T(8,128)S(1)}, f32[512,256]{1,0:T(8,128)S(1)}, f32[512,256]{1,0:T(8,128)S(1)}) custom-call(bf16[512,512]{1,0:T(8,128)(2,1)S(1)} %copy.48.q_ref, bf16[512,256]{1,0:T(8,128)(2,1)S(1)} %copy-done.3, bf16[512,256]{1,0:T(8,128)(2,1)S(1)} %copy-done.21, bf16[512,512]{1,0:T(8,128)(2,1)S(1)} %copy-done.16, ...), custom_call_target="tpu_custom_call" | custom-call | flops 1342177280 | bytes 2097152 | tf_op jit(solution)/shard_map/attend_back/pallas_call | solution.py:298
  259.4 1.7 fusion.144
  271.8 5.8 %boundary_bwd_last.1 = (f32[32,1024]{1,0:T(8,128)S(1)}, f32[1,1024]{1,0:T(1,128)S(1)}) custom-call(bf16[4,32,1024]{2,1,0:T(8,128)(2,1)S(1)} %bitcast.230, f32[32,1024]{1,0:T(8,128)S(1)} %bitcast.222, f32[1,1024]{1,0:T(1,128)S(1)} %get-tuple-element.143.refs_1_.refs_2_, f32[32,1024]{1,0:T(8,128)S(1)} %get-tuple-element.53.refs_3_), custom_call_target="tpu_custom_call" | custom-call | tf_op jit(solution)/shard_map/boundary_bwd_last/pallas_call | solution.py:175
  278.4 11.8 %sum_gains.1 = f32[40,128]{1,0:T(8,128)} custom-call(f32[40,128]{1,0:T(8,128)} %pad_bitcast_fusion.x_ref), custom_call_target="tpu_custom_call" | custom-call | tf_op jit(solution)/shard_map/sum_gains/pallas_call | solution.py:237
  291.7 2.0 fusion.57
  293.7 5.6 %boundary_fwd_last.1 = f32[32,1024]{1,0:T(8,128)S(1)} custom-call(bf16[4,32,1024]{2,1,0:T(8,128)(2,1)S(1)} %bitcast.236, f32[32,1024]{1,0:T(8,128)S(1)} %copy-done.1), custom_call_target="tpu_custom_call" | custom-call | tf_op jit(solution)/shard_map/boundary_fwd_last/pallas_call | solution.py:175
  (396 shorter events, 90.6 us)
Async XLA Ops:
  7.2 137.0 %all-gather.2.cloned.1.call-start = ((), (), s32[]{:S(2)}) async-start(), calls=%async_computation | async-start | bytes 1114112 | tf_op jit(solution)/shard_map/all_gather | solution.py:361
  11.1 38.3 %copy-start.94 = (f32[128]{0:T(128)}, f32[128]{0:T(128)S(1)}, u32[]{:S(2)}) copy-start(f32[128]{0:T(128)S(1)} %get-tuple-element.146) | copy-start | bytes 1540
  12.4 27.3 %copy-start.89 = (f32[128]{0:T(128)}, f32[128]{0:T(128)S(1)}, u32[]{:S(2)}) copy-start(f32[128]{0:T(128)S(1)} %get-tuple-element.145) | copy-start | bytes 1540
  16.6 34.1 %copy-start.24 = (f32[512,128]{0,1:T(8,128)}, f32[512,128]{0,1:T(8,128)S(1)}, u32[]{:S(2)}) copy-start(f32[512,128]{0,1:T(8,128)S(1)} %get-tuple-element.131) | copy-start | bytes 786436
  16.6 34.1 %copy-start.37 = (f32[512,128]{0,1:T(8,128)}, f32[512,128]{0,1:T(8,128)S(1)}, u32[]{:S(2)}) copy-start(f32[512,128]{0,1:T(8,128)S(1)} %get-tuple-element.130) | copy-start | bytes 786436
  54.8 25.8 %copy-start.50 = (bf16[2,1024,768]{2,1,0:T(8,128)(2,1)S(1)}, bf16[2,1024,768]{2,1,0:T(8,128)(2,1)}, u32[]{:S(2)}) copy-start(bf16[2,1024,768]{2,1,0:T(8,128)(2,1)} %param.22) | copy-start | bytes 9437188
  59.8 21.8 %copy-start.15 = (bf16[512,512]{1,0:T(8,128)(2,1)}, bf16[512,512]{1,0:T(8,128)(2,1)S(1)}, u32[]{:S(2)}) copy-start(bf16[512,512]{1,0:T(8,128)(2,1)S(1)} %attend.2.o_ref) | copy-start | bytes 1572868
  85.0 20.6 %copy-start.71 = (bf16[256,1024]{1,0:T(8,128)(2,1)S(1)}, bf16[256,1024]{1,0:T(8,128)(2,1)}, u32[]{:S(2)}) copy-start(bf16[256,1024]{1,0:T(8,128)(2,1)} %copy.32) | copy-start | bytes 1572868
  86.3 19.9 %copy-start.68 = (bf16[512,1024]{1,0:T(8,128)(2,1)S(1)}, bf16[512,1024]{1,0:T(8,128)(2,1)}, u32[]{:S(2)}) copy-start(bf16[512,1024]{1,0:T(8,128)(2,1)} %copy.30) | copy-start | bytes 3145732
  115.5 26.6 %copy-start.47 = (bf16[2,1024,768]{2,1,0:T(8,128)(2,1)S(1)}, bf16[2,1024,768]{2,1,0:T(8,128)(2,1)}, u32[]{:S(2)}) copy-start(bf16[2,1024,768]{2,1,0:T(8,128)(2,1)} %param.23) | copy-start | bytes 9437188
  119.9 24.3 %copy-start.17 = (bf16[512,512]{1,0:T(8,128)(2,1)}, bf16[512,512]{1,0:T(8,128)(2,1)S(1)}, u32[]{:S(2)}) copy-start(bf16[512,512]{1,0:T(8,128)(2,1)S(1)} %attend.3.o_ref) | copy-start | bytes 1572868
  140.9 14.2 %copy-start = (f32[32,1024]{1,0:T(8,128)}, f32[32,1024]{1,0:T(8,128)S(1)}, u32[]{:S(2)}) copy-start(f32[32,1024]{1,0:T(8,128)S(1)} %get-tuple-element.41.refs_1_) | copy-start | bytes 393220
  154.5 23.3 %copy-start.104 = (bf16[2,512,1024]{2,1,0:T(8,128)(2,1)S(1)}, bf16[2,512,1024]{2,1,0:T(8,128)(2,1)}, u32[]{:S(2)}) copy-start(bf16[2,512,1024]{2,1,0:T(8,128)(2,1)} %param.20) | copy-start | bytes 6291460
  194.1 21.7 %copy-start.101 = (bf16[2,768,1024]{2,1,0:T(8,128)(2,1)S(1)}, bf16[2,768,1024]{2,1,0:T(8,128)(2,1)}, u32[]{:S(2)}) copy-start(bf16[2,768,1024]{2,1,0:T(8,128)(2,1)} %param.24) | copy-start | bytes 9437188
  194.8 21.1 %copy-start.111 = (f32[512,768]{1,0:T(8,128)S(1)}, f32[512,768]{1,0:T(8,128)}, u32[]{:S(2)}) copy-start(f32[512,768]{1,0:T(8,128)} %get-tuple-element.153) | copy-start | bytes 4718596
  195.1 20.8 %copy-start.110 = (f32[512,768]{1,0:T(8,128)S(1)}, f32[512,768]{1,0:T(8,128)}, u32[]{:S(2)}) copy-start(f32[512,768]{1,0:T(8,128)} %copy-done.109) | copy-start | bytes 4718596
  221.4 20.9 %copy-start.105 = (bf16[2,512,1024]{2,1,0:T(8,128)(2,1)S(1)}, bf16[2,512,1024]{2,1,0:T(8,128)(2,1)}, u32[]{:S(2)}) copy-start(bf16[2,512,1024]{2,1,0:T(8,128)(2,1)} %param.20) | copy-start | bytes 6291460
  271.8 21.9 %copy-start.1 = (f32[32,1024]{1,0:T(8,128)S(1)}, f32[32,1024]{1,0:T(8,128)}, u32[]{:S(2)}) copy-start(f32[32,1024]{1,0:T(8,128)} %copy-done) | copy-start | bytes 393220
  300.2 19.9 %collective-permute-start.9 = (bf16[128,768]{1,0:T(8,128)(2,1)S(1)}, bf16[128,768]{1,0:T(8,128)(2,1)S(1)}, u32[]{:S(2)}, u32[]{:S(2)}) collective-permute-start(bf16[128,768]{1,0:T(8,128)(2,1)S(1)} %split.214), channel_id=1, source_target_pairs={{0,16},{16,0},{1,17},{17,1},{2,18},{18,2},{3,19},{19,3},{4,20},{20... | collective-permute-start | bytes 589832 | tf_op jit(solution)/shard_map/ppermute | solution.py:353
  300.3 22.0 %collective-permute-start.11 = (bf16[128,768]{1,0:T(8,128)(2,1)S(1)}, bf16[128,768]{1,0:T(8,128)(2,1)S(1)}, u32[]{:S(2)}, u32[]{:S(2)}) collective-permute-start(bf16[128,768]{1,0:T(8,128)(2,1)S(1)} %split.212), channel_id=1, source_target_pairs={{0,16},{16,0},{1,17},{17,1},{2,18},{18,2},{3,19},{19,3},{4,20},{20... | collective-permute-start | bytes 589832 | tf_op jit(solution)/shard_map/ppermute | solution.py:353
  301.2 12.8 %collective-permute-start.7 = (bf16[512,128]{1,0:T(8,128)(2,1)S(1)}, bf16[512,128]{1,0:T(8,128)(2,1)S(1)}, u32[]{:S(2)}, u32[]{:S(2)}) collective-permute-start(bf16[512,128]{1,0:T(8,128)(2,1)S(1)} %split.216), channel_id=1, source_target_pairs={{0,16},{16,0},{1,17},{17,1},{2,18},{18,2},{3,19},{19,3},{4,20},{20... | collective-permute-start | bytes 393224 | tf_op jit(solution)/shard_map/ppermute | solution.py:353
  303.5 16.7 %collective-permute-start.12 = (bf16[768,128]{1,0:T(8,128)(2,1)S(1)}, bf16[768,128]{1,0:T(8,128)(2,1)S(1)}, u32[]{:S(2)}, u32[]{:S(2)}) collective-permute-start(bf16[768,128]{1,0:T(8,128)(2,1)S(1)} %split.211), channel_id=1, source_target_pairs={{0,16},{16,0},{1,17},{17,1},{2,18},{18,2},{3,19},{19,3},{4,20},{20... | collective-permute-start | bytes 589832 | tf_op jit(solution)/shard_map/ppermute | solution.py:353
  304.5 4.1 %collective-permute-start.3 = (bf16[128,256]{1,0:T(8,128)(2,1)S(1)}, bf16[128,256]{1,0:T(8,128)(2,1)S(1)}, u32[]{:S(2)}, u32[]{:S(2)}) collective-permute-start(bf16[128,256]{1,0:T(8,128)(2,1)S(1)} %split.222), channel_id=1, source_target_pairs={{0,16},{16,0},{1,17},{17,1},{2,18},{18,2},{3,19},{19,3},{4,20},{20... | collective-permute-start | bytes 196616 | tf_op jit(solution)/shard_map/ppermute | solution.py:353
  308.6 1.3 collective-permute-start.5
  309.8 1.3 collective-permute-start.4
  311.1 1.3 collective-permute-start.2
  312.3 8.0 %collective-permute-start.13 = (bf16[768,128]{1,0:T(8,128)(2,1)S(1)}, bf16[768,128]{1,0:T(8,128)(2,1)S(1)}, u32[]{:S(2)}, u32[]{:S(2)}) collective-permute-start(bf16[768,128]{1,0:T(8,128)(2,1)S(1)} %split.210), channel_id=1, source_target_pairs={{0,16},{16,0},{1,17},{17,1},{2,18},{18,2},{3,19},{19,3},{4,20},{20... | collective-permute-start | bytes 589832 | tf_op jit(solution)/shard_map/ppermute | solution.py:353
  313.9 1.3 collective-permute-start.1
  315.3 1.3 collective-permute-start.6
  316.6 1.3 collective-permute-start
  318.0 2.4 collective-permute-start.8
  320.0 2.3 collective-permute-start.10
  (95 other events, 267.7 us)
Sparse Core Ops, SparseCore 0:
  11.3 59.4 all-gather.1

commit v2 on v1

--- a/solution.py
+++ b/solution.py
@@ -29,14 +29,8 @@
     half = head_dim // 2
     frequency = THETA ** (-(2.0 * jnp.arange(half, dtype=F32)) / head_dim)
     angles = positions[:, None] * frequency[None, :]
-    angles = jnp.concatenate([angles, angles], axis=-1)
-    return (jnp.cos(angles)[:, None, :], jnp.sin(angles)[:, None, :])
-
-
-def rotate(field, cosine, sine):
-    half = field.shape[-1] // 2
-    turned = jnp.concatenate([-field[..., half:], field[..., :half]], axis=-1)
-    return field * cosine + turned * sine
+    cosine, sine = jnp.cos(angles), jnp.sin(angles)
+    return (jnp.concatenate([cosine, cosine], axis=-1), jnp.concatenate([-sine, sine], axis=-1))
 
 
 def remote(src, dst, send, recv, **where):
@@ -71,11 +65,15 @@
     tp_peers = [lax.rem(me_t + d, n_tp) for d in range(1, n_tp)]
     ctx_peers = [lax.rem(me_c + d, n_ctx) for d in range(1, n_ctx)] if has_gather else []
     barrier = pltpu.get_barrier_semaphore()
-    for peer in tp_peers:
+    side = me_t + 1 - 2 * lax.rem(me_t, 2)
+    over = lax.rem(me_t + 2, n_tp)
+    cross = lax.rem(side + 2, n_tp)
+    greeted = tp_peers if has_sum else [side, over]
+    for peer in greeted:
         pl.semaphore_signal(barrier, inc=1, device_id={"tp": peer}, device_id_type=MESH)
     for peer in ctx_peers:
         pl.semaphore_signal(barrier, inc=1, device_id={"ctx": peer}, device_id_type=MESH)
-    pl.semaphore_wait(barrier, len(tp_peers) + len(ctx_peers))
+    pl.semaphore_wait(barrier, len(greeted) + len(ctx_peers))
 
     if has_sum:
         sums = [
@@ -108,33 +106,54 @@
 
     if has_gather:
         own[...] = sent
+        half = own.shape[0] // 2
+        order = sorted(range(1, n_ctx), key=lambda d: min(2 * d - 1, 2 * (n_ctx - d)))
         copies = []
-        for d, peer in enumerate(ctx_peers):
+        for d in order:
+            peer = ctx_peers[d - 1]
             copies.append(
-                remote(own, out.at[me_c, me_t], z_send.at[d], z_recv.at[d], ctx=peer)
+                remote(
+                    own, out.at[me_c, me_t], z_send.at[d - 1], z_recv.at[d - 1], ctx=peer
+                )
             )
-        for d, peer in enumerate(tp_peers):
-            copies.append(
-                remote(own, out.at[me_c, me_t], t_send.at[0, d], t_recv.at[0, d], tp=peer)
-            )
-        for copy in copies:
-            copy.start()
+            copies[-1].start()
+
+        def place(d, origin):
+            return out.at[lax.rem(me_c + n_ctx - d, n_ctx), origin]
+
+        def send(src, dst, d, k, peer):
+            copies.append(remote(src, dst, t_send.at[d, k], t_recv.at[d, k], tp=peer))
+            copies[-1].start()
+
+        def arrive(dst, d, k, peer):
+            remote(dst, dst, t_send.at[d, k], t_recv.at[d, k], tp=peer).wait_recv()
+
+        def spread(d):
+            src = own if d == 0 else place(d, me_t)
+            send(src, place(d, me_t), d, 0, side)
+            send(src, place(d, me_t), d, 1, over)
+
+        def relay(d):
+            arrive(place(d, side), d, 0, side)
+            upper = place(d, side).at[pl.ds(0, half)]
+            send(upper, upper, d, 2, over)
+            arrive(place(d, over), d, 1, over)
+            lower = place(d, over).at[pl.ds(half, half)]
+            send(lower, lower, d, 3, side)
+
+        spread(0)
         out[me_c, me_t] = sent
-        for d in range(n_ctx - 1):
-            source = lax.rem(me_c + n_ctx - (d + 1), n_ctx)
-            slot = out.at[source, me_t]
-            remote(own, slot, z_send.at[d], z_recv.at[d], ctx=source).wait_recv()
-            for k, peer in enumerate(tp_peers):
-                copy = remote(slot, slot, t_send.at[d + 1, k], t_recv.at[d + 1, k], tp=peer)
-                copy.start()
-                copies.append(copy)
-        for d in range(n_ctx):
+        behind = 0
+        for d in order:
             source = lax.rem(me_c + n_ctx - d, n_ctx)
-            for k in range(n_tp - 1):
-                origin = lax.rem(me_t + n_tp - (k + 1), n_tp)
-                remote(
-                    own, out.at[source, origin], t_send.at[d, k], t_recv.at[d, k], tp=origin
-                ).wait_recv()
+            remote(own, place(d, me_t), z_send.at[d - 1], z_recv.at[d - 1], ctx=source).wait_recv()
+            spread(d)
+            relay(behind)
+            behind = d
+        relay(behind)
+        for d in [0] + order:
+            arrive(place(d, cross).at[pl.ds(0, half)], d, 2, over)
+            arrive(place(d, cross).at[pl.ds(half, half)], d, 3, side)
         for copy in copies:
             copy.wait_send()
 
@@ -168,8 +187,8 @@
             pltpu.VMEM((rows, width), BF16),
             dma((n_ctx - 1,)),
             dma((n_ctx - 1,)),
-            dma((n_ctx, n_tp - 1)),
-            dma((n_ctx, n_tp - 1)),
+            dma((n_ctx, 4)),
+            dma((n_ctx, 4)),
         ]
     vmem = pl.BlockSpec(memory_space=pltpu.VMEM)
     outs = pl.pallas_call(
@@ -256,6 +275,15 @@
     return lax.dot_general(a, b, dims, preferred_element_type=F32)
 
 
+def turn(x):
+    return pltpu.roll(x, x.shape[-1] // 2, axis=1)
+
+
+def prepared(x, gain, cosine, sine):
+    normed, plain, inverse = rms_forward(x, gain)
+    return (normed * cosine + turn(normed) * sine).astype(BF16), plain, inverse
+
+
 def soft_weights(scale, bq, q, k):
     rows = pl.program_id(2) * bq + lax.broadcasted_iota(jnp.int32, (bq, k.shape[0]), 0)
     cols = lax.broadcasted_iota(jnp.int32, (bq, k.shape[0]), 1)
@@ -264,49 +292,119 @@
     return weights, jnp.sum(weights, axis=-1, keepdims=True)
 
 
-def attend_kernel(scale, bq, q_ref, k_ref, v_ref, o_ref):
-    weights, total = soft_weights(scale, bq, q_ref[...], k_ref[...])
+def attend_kernel(
+    scale, bq, q_ref, k_ref, v_ref, cq_ref, sq_ref, ck_ref, sk_ref, qg_ref, kg_ref, o_ref, k_rot
+):
+    @pl.when((pl.program_id(1) == 0) & (pl.program_id(2) == 0))
+    def _():
+        k_rot[...] = prepared(k_ref[...], kg_ref[...], ck_ref[...], sk_ref[...])[0]
+
+    q = prepared(q_ref[...], qg_ref[...], cq_ref[...], sq_ref[...])[0]
+    weights, total = soft_weights(scale, bq, q, k_rot[...])
     o_ref[...] = (dot(weights.astype(BF16), v_ref[...], NN) / total).astype(BF16)
 
 
-def attend_back_kernel(scale, bq, q_ref, k_ref, v_ref, o_ref, do_ref, dq_ref, dk_ref, dv_ref):
-    q, k, do = q_ref[...], k_ref[...], do_ref[...]
+def attend_back_kernel(
+    scale,
+    bq,
+    q_ref,
+    k_ref,
+    v_ref,
+    cq_ref,
+    sq_ref,
+    ck_ref,
+    sk_ref,
+    qg_ref,
+    kg_ref,
+    o_ref,
+    do_ref,
+    dq_ref,
+    dk_ref,
+    dv_ref,
+    qp_ref,
+    kp_ref,
+    k_rot,
+    dk_sum,
+    dv_sum,
+):
+    head, member, block = pl.program_id(0), pl.program_id(1), pl.program_id(2)
+
+    @pl.when((head == 0) & (member == 0) & (block == 0))
+    def _():
+        qp_ref[...] = jnp.zeros_like(qp_ref)
+        kp_ref[...] = jnp.zeros_like(kp_ref)
+
+    @pl.when((member == 0) & (block == 0))
+    def _():
+        k_rot[...] = prepared(k_ref[...], kg_ref[...], ck_ref[...], sk_ref[...])[0]
+        dk_sum[...] = jnp.zeros_like(dk_sum)
+        dv_sum[...] = jnp.zeros_like(dv_sum)
+
+    q, plain, inverse = prepared(q_ref[...], qg_ref[...], cq_ref[...], sq_ref[...])
+    k, do = k_rot[...], do_ref[...]
     weights, total = soft_weights(scale, bq, q, k)
     probs = weights / total
     delta = jnp.sum(do.astype(F32) * o_ref[...].astype(F32), axis=-1, keepdims=True)
     dscore = (probs * (dot(do, v_ref[...], NT) - delta)).astype(BF16)
-    dq_ref[...] = dot(dscore, k, NN) * scale
-
-    @pl.when((pl.program_id(1) == 0) & (pl.program_id(2) == 0))
+    dk_sum[...] += dot(dscore, q, TN) * scale
+    dv_sum[...] += dot(probs.astype(BF16), do, TN)
+    grad = dot(dscore, k, NN) * scale
+    grad = grad * cq_ref[...] - turn(grad) * sq_ref[...]
+    qp_ref[...] += jnp.sum(grad * plain, axis=0, keepdims=True)
+    dq_ref[...] = rms_backward(grad, plain, inverse, qg_ref[...]).astype(BF16)
+
+    @pl.when((member == pl.num_programs(1) - 1) & (block == pl.num_programs(2) - 1))
     def _():
-        dk_ref[...] = jnp.zeros_like(dk_ref)
-        dv_ref[...] = jnp.zeros_like(dv_ref)
-
-    dk_ref[...] += dot(dscore, q, TN) * scale
-    dv_ref[...] += dot(probs.astype(BF16), do, TN)
-
-
-def attention(back, scale, group, head_dim, *operands):
-    length, kv_width = operands[1].shape
+        _, k_plain, k_inverse = prepared(k_ref[...], kg_ref[...], ck_ref[...], sk_ref[...])
+        grad_k = dk_sum[...]
+        grad_k = grad_k * ck_ref[...] - turn(grad_k) * sk_ref[...]
+        kp_ref[...] += jnp.sum(grad_k * k_plain, axis=0, keepdims=True)
+        dk_ref[...] = rms_backward(grad_k, k_plain, k_inverse, kg_ref[...]).astype(BF16)
+        dv_ref[...] = dv_sum[...].astype(BF16)
+
+
+def attention(scale, group, query, keys, values, cosine, sine, query_gain, key_gain, *back):
+    length, kv_width = keys.shape
+    head_dim = cosine.shape[-1]
     kv_heads = kv_width // head_dim
     bq = min(length, 256)
     rows = pl.BlockSpec((bq, head_dim), lambda h, g, i: (i, h * group + g))
-    keys = pl.BlockSpec((length, head_dim), lambda h, g, i: (0, h))
-    wide = jax.ShapeDtypeStruct((length, kv_width * group), F32 if back else BF16)
-    narrow = jax.ShapeDtypeStruct((length, kv_width), F32)
+    keyed = pl.BlockSpec((length, head_dim), lambda h, g, i: (0, h))
+    table_q = pl.BlockSpec((bq, head_dim), lambda h, g, i: (i, 0))
+    table_k = pl.BlockSpec((length, head_dim), lambda h, g, i: (0, 0))
+    flat = pl.BlockSpec((1, head_dim), lambda h, g, i: (0, 0))
+    wide = jax.ShapeDtypeStruct((length, kv_width * group), BF16)
+    narrow = jax.ShapeDtypeStruct((length, kv_width), BF16)
+    part = jax.ShapeDtypeStruct((1, head_dim), F32)
     work = 2 * length * length * head_dim * kv_heads * group
+    scratch = [pltpu.VMEM((length, head_dim), BF16)]
+    if back:
+        scratch += [pltpu.VMEM((length, head_dim), F32)] * 2
     return pl.pallas_call(
         functools.partial(attend_back_kernel if back else attend_kernel, scale, bq),
         grid=(kv_heads, group, length // bq),
-        out_shape=(wide, narrow, narrow) if back else wide,
-        in_specs=[rows, keys, keys] + ([rows, rows] if back else []),
-        out_specs=(rows, keys, keys) if back else rows,
+        out_shape=(wide, narrow, narrow, part, part) if back else wide,
+        in_specs=[rows, keyed, keyed, table_q, table_q, table_k, table_k, flat, flat]
+        + [rows] * len(back),
+        out_specs=(rows, keyed, keyed, flat, flat) if back else rows,
+        scratch_shapes=scratch,
         name="attend_back" if back else "attend",
         cost_estimate=pl.CostEstimate(
             flops=work * (5 if back else 2), bytes_accessed=4 * length * 1024, transcendentals=0
         ),
-        compiler_params=pltpu.CompilerParams(vmem_limit_bytes=32 * 2**20),
-    )(*operands)
+        compiler_params=pltpu.CompilerParams(vmem_limit_bytes=40 * 2**20),
+    )(
+        query,
+        keys,
+        values,
+        cosine,
+        sine,
+        cosine,
+        sine,
+        query_gain.reshape(1, -1),
+        key_gain.reshape(1, -1),
+        *back,
+    )
 
 
 def on_device(
@@ -325,7 +423,7 @@
     grad_output,
 ):
     local_rows, seq_local, width = block_input.shape
-    assert seq_local == 1 and lax.axis_size("dp") == 2
+    assert seq_local == 1 and lax.axis_size("dp") == 2 and lax.axis_size("tp") == 4
     layers = input_gain.shape[0]
     head_dim = query_gain.shape[-1]
     heads = query_weight.shape[-1] // head_dim
@@ -352,10 +450,16 @@
         own, other = jnp.split(grad, 2, axis=axis)
         return own + lax.ppermute(other.astype(BF16), "dp", swap).astype(F32)
 
-    def heads_of(x, count):
-        return x.reshape(length, count, head_dim)
-
-    attend_args = (scale, heads // kv_heads, head_dim)
+    def settle_rows(*products):
+        other = [x[piece:].astype(BF16) for x in products]
+        other = lax.ppermute(jnp.concatenate(other, axis=1), "dp", swap).astype(F32)
+        out = []
+        at = 0
+        for x in products:
+            out.append(x[:piece] + other[:, at : at + x.shape[1]])
+            at += x.shape[1]
+        return out
+
     hidden = block_input[:, 0]
     grad_hidden = grad_output[:, 0]
     grad_rows = lax.all_gather(grad_hidden.astype(BF16), ("ctx", "tp"), axis=0, tiled=True)
@@ -365,11 +469,9 @@
         query = dot(first_in, query_weight[l], NN)
         keys = dot(first_in, key_weight[l], NN)
         values = dot(first_in, value_weight[l], NN).astype(BF16)
-        query_normed, q_plain, q_inv = rms_forward(heads_of(query, heads), query_gain[l])
-        key_normed, k_plain, k_inv = rms_forward(heads_of(keys, kv_heads), key_gain[l])
-        query_rot = rotate(query_normed, cosine, sine).astype(BF16).reshape(length, -1)
-        key_rot = rotate(key_normed, cosine, sine).astype(BF16).reshape(length, -1)
-        attended = attention(False, *attend_args, query_rot, key_rot, values)
+        attend_args = (scale, heads // kv_heads, query, keys, values, cosine, sine)
+        attend_args += (query_gain[l], key_gain[l])
+        attended = attention(*attend_args)
         partial = dot(mine(attended), out_weight[l], NN).astype(BF16)
         mixed, second_in = boundary("fwd", hidden, post_gain[l], partial)
         gate = dot(second_in, gate_weight[l], NN)
@@ -377,19 +479,19 @@
         swish = (jax.nn.silu(gate) * upward).astype(BF16)
         partial = dot(mine(swish), down_weight[l], NN).astype(BF16)
         kept.append(
-            (hidden, first_in, q_plain, q_inv, k_plain, k_inv, query_rot, key_rot, values)
-            + (attended, mixed, second_in, gate, upward, swish)
+            (hidden, first_in, attend_args, attended, mixed, second_in, gate, upward, swish)
         )
         if l + 1 < layers:
             hidden, first_in = boundary("fwd", mixed, input_gain[l + 1], partial)
         else:
-            (hidden,) = boundary("fwd_last", mixed, None, partial)
+            hidden = mixed + lax.psum_scatter(
+                partial, "tp", scatter_dimension=0, tiled=True
+            ).astype(F32)
 
     grads = [None] * layers
     gains = [None] * layers
     for l in reversed(range(layers)):
-        (x_in, first_in, q_plain, q_inv, k_plain, k_inv, query_rot, key_rot, values) = kept[l][:9]
-        attended, mixed, second_in, gate, upward, swish = kept[l][9:]
+        x_in, first_in, attend_args, attended, mixed, second_in, gate, upward, swish = kept[l]
         grad_swish = dot(grad_rows, down_weight[l], NT)
         sigma = jax.nn.sigmoid(gate)
         grad_gate = (grad_swish * upward * (sigma * (1.0 + gate * (1.0 - sigma)))).astype(BF16)
@@ -400,23 +502,13 @@
         )
         second_cols = slices(second_in)
         down_grad = settle(dot(swish, slices(grad_rows), TN), 1)
-        gate_grad = settle(dot(second_cols, grad_gate, TN), 0)
-        up_grad = settle(dot(second_cols, grad_up, TN), 0)
+        gate_grad, up_grad = settle_rows(
+            dot(second_cols, grad_gate, TN), dot(second_cols, grad_up, TN)
+        )
 
         grad_heads = dot(mixed_rows, out_weight[l], NT).astype(BF16)
         out_grad = settle(dot(attended, slices(mixed_rows), TN), 1)
-        grad_query, grad_keys, grad_values = attention(
-            True, *attend_args, query_rot, key_rot, values, attended, grad_heads
-        )
-        grad_query = rotate(heads_of(grad_query, heads), cosine, -sine)
-        grad_keys = rotate(heads_of(grad_keys, kv_heads), cosine, -sine)
-        q_part = jnp.sum(mine(grad_query * q_plain), axis=(0, 1))
-        k_part = jnp.sum(mine(grad_keys * k_plain), axis=(0, 1))
-        query_bf = rms_backward(grad_query, q_plain, q_inv, query_gain[l]).astype(BF16)
-        key_bf = rms_backward(grad_keys, k_plain, k_inv, key_gain[l]).astype(BF16)
-        query_bf = query_bf.reshape(length, -1)
-        key_bf = key_bf.reshape(length, -1)
-        value_bf = grad_values.astype(BF16)
+        query_bf, key_bf, value_bf, q_part, k_part = attention(*attend_args, attended, grad_heads)
         partial = (
             dot(mine(query_bf), query_weight[l], NT)
             + dot(mine(key_bf), key_weight[l], NT)
@@ -431,11 +523,13 @@
                 "bwd_last", x_in, input_gain[l], partial, grad_mixed
             )
         first_cols = slices(first_in)
-        query_grad = settle(dot(first_cols, query_bf, TN), 0)
-        key_grad = settle(dot(first_cols, key_bf, TN), 0)
-        value_grad = settle(dot(first_cols, value_bf, TN), 0)
+        query_grad, key_grad, value_grad = settle_rows(
+            dot(first_cols, query_bf, TN),
+            dot(first_cols, key_bf, TN),
+            dot(first_cols, value_bf, TN),
+        )
         grads[l] = (query_grad, key_grad, value_grad, out_grad, gate_grad, up_grad, down_grad)
-        gains[l] = (input_part[0], q_part, k_part, post_part[0])
+        gains[l] = (input_part[0], q_part[0] / n_ctx, k_part[0] / n_ctx, post_part[0])
     stacked = [jnp.stack([part[m] for part in grads]) for m in range(7)]
     packed = jnp.concatenate([v for part in gains for v in part])
     sizes = [v.shape[0] for part in gains for v in part]

time: 331 us -> 315 us (0.952)
  Pallas kernels: 185 us -> 205 us
  local copies, waits for them, and re-layouts: 43.9 us -> 26.6 us
  other arithmetic: 27.1 us -> 13 us
  matrix products: 48 us -> 43.6 us
    pallas_call x4, Pallas kernels: 25.9 us -> 36.7 us  [attention(): pl.pallas_call(functools.partial(attend_back_kernel if back else attend_k...]
    pallas_call x9 -> x8, Pallas kernels: 148 us -> 157 us  [boundary(): pl.pallas_call(functools.partial(boundary_kernel, mode, n_ctx, n_tp), out...]
    dot_general x6 -> x0, local copies, waits for them, and re-layouts: 8.52 us -> none  [dot(): return lax.dot_general(a, b, dims, preferred_element_type=F32)]
    reduce_scatter x0 -> x1, waiting for transfers between devices: none -> 7.04 us  [on_device(): lax.psum_scatter(partial, 'tp', scatter_dimension=0, tiled=True).astype(F32)]
    reshape x8 -> x0, local copies, waits for them, and re-layouts: 5.58 us -> none  [the longest x4 3.85 us: heads_of(): return x.reshape(length, count, head_dim)]
    mul x5 -> x0, other arithmetic: 5.29 us -> none  [the longest x4 5.21 us: rms_forward(): return (normed * gain, normed, inverse)]
    reduce_sum x6 -> x0, other arithmetic: 5.24 us -> none  [the longest x4 2.35 us: rms_backward(): jnp.mean(scaled * normed, axis=-1, keepdims=True)]
    ppermute x14 -> x4, waiting for transfers between devices: 6.16 us -> 1.09 us  [settle(): return own + lax.ppermute(other.astype(BF16), 'dp', swap).astype(F32)]
  transfers between devices with their start and end apart: 15 -> 10, of which waited for: 6 -> 3; matrix products, arithmetic and copies ran while one was open for 16% -> 11% of each run, Pallas kernels for 27% -> 32%
where the time goes in v2:
time: 315 us; the launch traced here: 314 us
  Pallas kernels  205 us (65%)
  matrix products  43.6 us (14%)
  local copies, waits for them, and re-layouts  26.6 us (8%)
  between operations  15.3 us (5%)
  other arithmetic  13 us (4%)
  waiting for transfers between devices  8.26 us (3%)
    pallas_call x8, Pallas kernels, boundary(): pl.pallas_call(functools.partial(boundary_kernel, mode, n_ctx, n_tp), out...  157 us
    dot_general x42, matrix products, dot(): return lax.dot_general(a, b, dims, preferred_element_type=F32)  43.6 us
    pallas_call x4, Pallas kernels, attention(): pl.pallas_call(functools.partial(attend_back_kernel if back else attend_k...  36.7 us
    unnamed x176, local copies, waits for them, and re-layouts  13.9 us
    pallas_call x1, Pallas kernels, sum_gains(): pl.pallas_call(functools.partial(gains_kernel, sizes), out_shape=jax.Shap...  11.7 us
    dynamic_slice x7, local copies, waits for them, and re-layouts, slices(): lax.dynamic_slice_in_dim(x, at, piece, 1)  7.65 us
    reduce_scatter x1, waiting for transfers between devices, on_device(): lax.psum_scatter(partial, 'tp', scatter_dimension=0, tiled=True).astype(F32)  7.04 us
    another operation x17, other arithmetic, on_device(): stacked = [jnp.stack([part[m] for part in grads]) for m in range(7)]  6.36 us
  transfers between devices with their start and end apart: 10, of which 3 were waited for; matrix products, arithmetic and copies ran while one was open for 11% of the time, Pallas kernels for 32%

profile of v2, /device:TPU:0, one launch (start us, length us, event | category | flops | bytes accessed | tf_op | source)
XLA Modules:
  0.0 314.1 jit_solution(1450559828157465886)
XLA Ops:
  7.2 1.6 copy.48
  11.5 1.7 fusion.146
  13.2 21.2 %boundary_first.1 = bf16[4,4,32,1024]{3,2,1,0:T(8,128)(2,1)S(1)} custom-call(f32[32,1024]{1,0:T(8,128)S(1)} %bitcast.188, f32[1,1024]{1,0:T(1,128)S(1)} %get-tuple-element.120.refs_1_.refs_2_), custom_call_target="tpu_custom_call" | custom-call | tf_op jit(solution)/shard_map/boundary_first/pallas_call | solution.py:194
  38.0 1.4 pad_maximum_fusion.7
  39.4 6.2 %attend.2.o_ref = bf16[512,512]{1,0:T(8,128)(2,1)S(1)} custom-call(f32[512,512]{1,0:T(8,128)S(1)} %fusion.68.q_ref, f32[512,256]{1,0:T(8,128)S(1)} %copy-done.5, bf16[512,256]{1,0:T(8,128)(2,1)S(1)} %convolution_convert_fusion.5.v_ref, f32[512,128]{1,0:T(8,128)S(1)} %get-tuple-element.130.cq_ref.ck_ref, f32[512,128]{1,0:T(8,128)S(1)} %get-tuple-element.131.sq_ref.sk_ref, ...), custom_call_target="tpu_custom_call" | custom-call | flops 536870912 | bytes 2097152 | tf_op jit(solution)/shard_map/attend/pallas_call | solution.py:383
  46.0 22.9 %boundary_fwd.3 = (f32[32,1024]{1,0:T(8,128)S(1)}, bf16[4,4,32,1024]{3,2,1,0:T(8,128)(2,1)S(1)}) custom-call(bf16[4,32,1024]{2,1,0:T(8,128)(2,1)S(1)} %bitcast.202, f32[32,1024]{1,0:T(8,128)S(1)} %bitcast.189, f32[1,1024]{1,0:T(1,128)S(1)} %get-tuple-element.118.refs_2_), custom_call_target="tpu_custom_call" | custom-call | tf_op jit(solution)/shard_map/boundary_fwd/pallas_call | solution.py:194
  69.9 1.3 copy-done.29
  71.2 2.2 multiply_convert_fusion.5
  76.9 22.0 %boundary_fwd.4 = (f32[32,1024]{1,0:T(8,128)S(1)}, bf16[4,4,32,1024]{3,2,1,0:T(8,128)(2,1)S(1)}) custom-call(bf16[4,32,1024]{2,1,0:T(8,128)(2,1)S(1)} %bitcast.200, f32[32,1024]{1,0:T(8,128)S(1)} %get-tuple-element.41.refs_1_, f32[1,1024]{1,0:T(1,128)S(1)} %get-tuple-element.119.refs_2_), custom_call_target="tpu_custom_call" | custom-call | tf_op jit(solution)/shard_map/boundary_fwd/pallas_call | solution.py:194
  98.9 1.5 convolution_convert_fusion.3.v_ref
  102.9 6.4 %attend.3.o_ref = bf16[512,512]{1,0:T(8,128)(2,1)S(1)} custom-call(f32[512,512]{1,0:T(8,128)S(1)} %fusion.63.q_ref, f32[512,256]{1,0:T(8,128)S(1)} %fusion.83.k_ref, bf16[512,256]{1,0:T(8,128)(2,1)S(1)} %convolution_convert_fusion.3.v_ref, f32[512,128]{1,0:T(8,128)S(1)} %get-tuple-element.130.cq_ref.ck_ref, f32[512,128]{1,0:T(8,128)S(1)} %get-tuple-element.131.sq_ref.sk_ref, ...), custom_call_target="tpu_custom_call" | custom-call | flops 536870912 | bytes 2097152 | tf_op jit(solution)/shard_map/attend/pallas_call | solution.py:383
  109.7 20.6 %boundary_fwd.5 = (f32[32,1024]{1,0:T(8,128)S(1)}, bf16[4,4,32,1024]{3,2,1,0:T(8,128)(2,1)S(1)}) custom-call(bf16[4,32,1024]{2,1,0:T(8,128)(2,1)S(1)} %bitcast.201, f32[32,1024]{1,0:T(8,128)S(1)} %get-tuple-element.43.refs_1_, f32[1,1024]{1,0:T(1,128)S(1)} %get-tuple-element.117.refs_2_), custom_call_target="tpu_custom_call" | custom-call | tf_op jit(solution)/shard_map/boundary_fwd/pallas_call | solution.py:194
  131.0 2.0 constant_dynamic-slice_fusion.7
  134.5 2.2 fusion.6
  136.7 2.9 fusion
  139.7 4.0 %multiply_convert_fusion.3 = (bf16[512,768]{1,0:T(8,128)(2,1)S(1)}, bf16[512,768]{1,0:T(8,128)(2,1)S(1)}, bf16[512,768]{1,0:T(8,128)(2,1)}) fusion(f32[512,768]{1,0:T(8,128)S(1)} %fusion, f32[512,768]{1,0:T(8,128)} %fusion.6, bf16[512,1024]{1,0:T(8,128)(2,1)S(1)} %bitcast.209, bf16[2,1024,768]{2,1,0:T(8,128)(2,1)S(1)} %copy-done.33), kind=kOutput, calls=%fused_computation.27 | convolution fusion | flops 811204608 | bytes 8126464 | tf_op jit(solution)/shard_map/dot_general | solution.py:275
  144.7 1.3 fusion.134
  146.0 1.3 fusion.135
  148.2 21.3 %boundary_bwd.3 = (f32[32,1024]{1,0:T(8,128)S(1)}, f32[1,1024]{1,0:T(1,128)S(1)}, bf16[4,4,32,1024]{3,2,1,0:T(8,128)(2,1)S(1)}) custom-call(bf16[4,32,1024]{2,1,0:T(8,128)(2,1)S(1)} %bitcast.196, f32[32,1024]{1,0:T(8,128)S(1)} %copy-done.10, f32[1,1024]{1,0:T(1,128)S(1)} %get-tuple-element.117.refs_2_, f32[32,1024]{1,0:T(8,128)S(1)} %bitcast.199), custom_call_target="tpu_custom_call" | custom-call | tf_op jit(solution)/shard_map/boundary_bwd/pallas_call | solution.py:194
  171.9 12.0 %attend_back.2 = (bf16[512,512]{1,0:T(8,128)(2,1)S(1)}, bf16[512,256]{1,0:T(8,128)(2,1)S(1)}, bf16[512,256]{1,0:T(8,128)(2,1)S(1)}, f32[1,128]{1,0:T(1,128)S(1)}, f32[1,128]{1,0:T(1,128)S(1)}) custom-call(f32[512,512]{1,0:T(8,128)S(1)} %copy-done.1, f32[512,256]{1,0:T(8,128)S(1)} %copy-done.8, bf16[512,256]{1,0:T(8,128)(2,1)S(1)} %copy-done.16, ...), custom_call_target="tpu_custom_call" | custom-call | flops 1342177280 | bytes 2097152 | tf_op jit(solution)/shard_map/attend_back/pallas_call | solution.py:383
  188.2 22.1 %boundary_bwd.4 = (f32[32,1024]{1,0:T(8,128)S(1)}, f32[1,1024]{1,0:T(1,128)S(1)}, bf16[4,4,32,1024]{3,2,1,0:T(8,128)(2,1)S(1)}) custom-call(bf16[4,32,1024]{2,1,0:T(8,128)(2,1)S(1)} %bitcast.195, f32[32,1024]{1,0:T(8,128)S(1)} %get-tuple-element.43.refs_1_, f32[1,1024]{1,0:T(1,128)S(1)} %get-tuple-element.119.refs_2_, f32[32,1024]{1,0:T(8,128)S(1)} %get-tuple-element.50.refs_3_), custom_call_target="tpu_custom_call" | custom-call | tf_op jit(solution)/shard_map/boundary_bwd/pallas_call | solution.py:194
  211.1 2.9 multiply_convert_fusion.1
  215.0 1.3 fusion.136
  216.3 1.4 fusion.137
  218.3 21.0 %boundary_bwd.5 = (f32[32,1024]{1,0:T(8,128)S(1)}, f32[1,1024]{1,0:T(1,128)S(1)}, bf16[4,4,32,1024]{3,2,1,0:T(8,128)(2,1)S(1)}) custom-call(bf16[4,32,1024]{2,1,0:T(8,128)(2,1)S(1)} %bitcast.197, f32[32,1024]{1,0:T(8,128)S(1)} %get-tuple-element.41.refs_1_, f32[1,1024]{1,0:T(1,128)S(1)} %get-tuple-element.118.refs_2_, f32[32,1024]{1,0:T(8,128)S(1)} %get-tuple-element.52.refs_3_), custom_call_target="tpu_custom_call" | custom-call | tf_op jit(solution)/shard_map/boundary_bwd/pallas_call | solution.py:194
  241.2 12.0 %attend_back.3 = (bf16[512,512]{1,0:T(8,128)(2,1)S(1)}, bf16[512,256]{1,0:T(8,128)(2,1)S(1)}, bf16[512,256]{1,0:T(8,128)(2,1)S(1)}, f32[1,128]{1,0:T(1,128)S(1)}, f32[1,128]{1,0:T(1,128)S(1)}) custom-call(f32[512,512]{1,0:T(8,128)S(1)} %fusion.68.q_ref, f32[512,256]{1,0:T(8,128)S(1)} %copy-done.6, bf16[512,256]{1,0:T(8,128)(2,1)S(1)} %copy-done.14, ...), custom_call_target="tpu_custom_call" | custom-call | flops 1342177280 | bytes 2097152 | tf_op jit(solution)/shard_map/attend_back/pallas_call | solution.py:383
  253.5 1.8 constant_dynamic-slice_fusion.1
  259.2 5.9 %boundary_bwd_last.1 = (f32[32,1024]{1,0:T(8,128)S(1)}, f32[1,1024]{1,0:T(1,128)S(1)}) custom-call(bf16[4,32,1024]{2,1,0:T(8,128)(2,1)S(1)} %bitcast.198, f32[32,1024]{1,0:T(8,128)S(1)} %bitcast.190, f32[1,1024]{1,0:T(1,128)S(1)} %get-tuple-element.120.refs_1_.refs_2_, f32[32,1024]{1,0:T(8,128)S(1)} %get-tuple-element.57.refs_3_), custom_call_target="tpu_custom_call" | custom-call | tf_op jit(solution)/shard_map/boundary_bwd_last/pallas_call | solution.py:194
  265.8 11.7 %sum_gains.1 = f32[40,128]{1,0:T(8,128)} custom-call(f32[40,128]{1,0:T(8,128)} %pad_bitcast_fusion.x_ref), custom_call_target="tpu_custom_call" | custom-call | tf_op jit(solution)/shard_map/sum_gains/pallas_call | solution.py:256
  277.4 1.3 fusion.187
  279.6 2.6 fusion.57
  298.6 7.0 %reduce-scatter.2.cloned.1.call-done = bf16[32,1024]{1,0:T(8,128)(2,1)} async-done(((bf16[128,1024]{1,0:T(8,128)(2,1)}), bf16[32,1024]{1,0:T(8,128)(2,1)}) %reduce-scatter.2.cloned.1.call-update) | async-done | bytes 65552 | tf_op jit(solution)/shard_map/reduce_scatter | solution.py:487
  (286 shorter events, 52.0 us)
Async XLA Ops:
  7.2 27.2 %copy-start.47 = (bf16[2,1024,256]{2,1,0:T(8,128)(2,1)S(1)}, bf16[2,1024,256]{2,1,0:T(8,128)(2,1)}, u32[]{:S(2)}) copy-start(bf16[2,1024,256]{2,1,0:T(8,128)(2,1)} %param.17) | copy-start | bytes 3145732
  7.2 129.5 %all-gather.2.cloned.1.call-start = ((), (), s32[]{:S(2)}) async-start(), calls=%async_computation.2 | async-start | bytes 1114112 | tf_op jit(solution)/shard_map/all_gather | solution.py:465
  8.9 296.7 %reduce-scatter.2.cloned.1.call-start = ((), (), s32[]{:S(2)}) async-start(), calls=%async_computation.1 | async-start | bytes 327680 | tf_op jit(solution)/shard_map/reduce_scatter | solution.py:487
  13.2 21.6 %copy-start.49 = (bf16[2,1024,256]{2,1,0:T(8,128)(2,1)S(1)}, bf16[2,1024,256]{2,1,0:T(8,128)(2,1)}, u32[]{:S(2)}) copy-start(bf16[2,1024,256]{2,1,0:T(8,128)(2,1)} %param.16) | copy-start | bytes 3145732
  38.0 7.7 %copy-start.21 = (f32[1,128]{1,0:T(1,128)}, f32[1,128]{1,0:T(1,128)S(1)}, u32[]{:S(2)}) copy-start(f32[1,128]{1,0:T(1,128)S(1)} %get-tuple-element.122.kg_ref) | copy-start | bytes 1540
  38.0 7.7 %copy-start.23 = (f32[1,128]{1,0:T(1,128)}, f32[1,128]{1,0:T(1,128)S(1)}, u32[]{:S(2)}) copy-start(f32[1,128]{1,0:T(1,128)S(1)} %get-tuple-element.132.qg_ref) | copy-start | bytes 1540
  38.0 7.7 %copy-start.75 = (bf16[2,512,1024]{2,1,0:T(8,128)(2,1)S(1)}, bf16[2,512,1024]{2,1,0:T(8,128)(2,1)}, u32[]{:S(2)}) copy-start(bf16[2,512,1024]{2,1,0:T(8,128)(2,1)} %param.20) | copy-start | bytes 6291460
  39.4 29.5 %copy-start.32 = (bf16[2,1024,768]{2,1,0:T(8,128)(2,1)S(1)}, bf16[2,1024,768]{2,1,0:T(8,128)(2,1)}, u32[]{:S(2)}) copy-start(bf16[2,1024,768]{2,1,0:T(8,128)(2,1)} %param.22) | copy-start | bytes 9437188
  76.9 23.5 %copy-start.50 = (bf16[2,1024,256]{2,1,0:T(8,128)(2,1)S(1)}, bf16[2,1024,256]{2,1,0:T(8,128)(2,1)}, u32[]{:S(2)}) copy-start(bf16[2,1024,256]{2,1,0:T(8,128)(2,1)} %param.16) | copy-start | bytes 3145732
  102.8 6.5 %copy-start = (f32[512,512]{1,0:T(8,128)}, f32[512,512]{1,0:T(8,128)S(1)}, u32[]{:S(2)}) copy-start(f32[512,512]{1,0:T(8,128)S(1)} %fusion.63.q_ref) | copy-start | bytes 3145732
  102.9 6.4 %copy-start.76 = (bf16[2,512,1024]{2,1,0:T(8,128)(2,1)S(1)}, bf16[2,512,1024]{2,1,0:T(8,128)(2,1)}, u32[]{:S(2)}) copy-start(bf16[2,512,1024]{2,1,0:T(8,128)(2,1)} %param.20) | copy-start | bytes 6291460
  109.3 25.2 %copy-start.2 = (bf16[512,512]{1,0:T(8,128)(2,1)}, bf16[512,512]{1,0:T(8,128)(2,1)S(1)}, u32[]{:S(2)}) copy-start(bf16[512,512]{1,0:T(8,128)(2,1)S(1)} %attend.3.o_ref) | copy-start | bytes 1572868
  109.3 25.2 %copy-start.30 = (bf16[2,1024,768]{2,1,0:T(8,128)(2,1)S(1)}, bf16[2,1024,768]{2,1,0:T(8,128)(2,1)}, u32[]{:S(2)}) copy-start(bf16[2,1024,768]{2,1,0:T(8,128)(2,1)} %param.23) | copy-start | bytes 9437188
  147.3 23.1 %copy-start.77 = (bf16[2,512,1024]{2,1,0:T(8,128)(2,1)S(1)}, bf16[2,512,1024]{2,1,0:T(8,128)(2,1)}, u32[]{:S(2)}) copy-start(bf16[2,512,1024]{2,1,0:T(8,128)(2,1)} %param.20) | copy-start | bytes 6291460
  171.9 12.0 %copy-start.48 = (bf16[2,1024,256]{2,1,0:T(8,128)(2,1)S(1)}, bf16[2,1024,256]{2,1,0:T(8,128)(2,1)}, u32[]{:S(2)}) copy-start(bf16[2,1024,256]{2,1,0:T(8,128)(2,1)} %param.17) | copy-start | bytes 3145732
  171.9 12.4 %copy-start.53 = (bf16[512,128]{1,0:T(8,128)(2,1)S(1)}, bf16[512,128]{1,0:T(8,128)(2,1)}, u32[]{:S(2)}) copy-start(bf16[512,128]{1,0:T(8,128)(2,1)} %get-tuple-element.99) | copy-start | bytes 393220
  171.9 12.4 %copy-start.54 = (bf16[512,128]{1,0:T(8,128)(2,1)S(1)}, bf16[512,128]{1,0:T(8,128)(2,1)}, u32[]{:S(2)}) copy-start(bf16[512,128]{1,0:T(8,128)(2,1)} %get-tuple-element.100) | copy-start | bytes 393220
  186.6 24.5 %copy-start.83 = (f32[512,768]{1,0:T(8,128)S(1)}, f32[512,768]{1,0:T(8,128)}, u32[]{:S(2)}) copy-start(f32[512,768]{1,0:T(8,128)} %copy-done.82) | copy-start | bytes 4718596
  187.7 23.4 %copy-start.74 = (bf16[2,768,1024]{2,1,0:T(8,128)(2,1)S(1)}, bf16[2,768,1024]{2,1,0:T(8,128)(2,1)}, u32[]{:S(2)}) copy-start(bf16[2,768,1024]{2,1,0:T(8,128)(2,1)} %param.24) | copy-start | bytes 9437188
  217.7 22.4 %copy-start.78 = (bf16[2,512,1024]{2,1,0:T(8,128)(2,1)S(1)}, bf16[2,512,1024]{2,1,0:T(8,128)(2,1)}, u32[]{:S(2)}) copy-start(bf16[2,512,1024]{2,1,0:T(8,128)(2,1)} %param.20) | copy-start | bytes 6291460
  259.2 23.1 %copy-start.59 = (bf16[512,128]{1,0:T(8,128)(2,1)S(1)}, bf16[512,128]{1,0:T(8,128)(2,1)}, u32[]{:S(2)}) copy-start(bf16[512,128]{1,0:T(8,128)(2,1)} %get-tuple-element.87) | copy-start | bytes 393220
  259.2 23.1 %copy-start.60 = (bf16[512,128]{1,0:T(8,128)(2,1)S(1)}, bf16[512,128]{1,0:T(8,128)(2,1)}, u32[]{:S(2)}) copy-start(bf16[512,128]{1,0:T(8,128)(2,1)} %get-tuple-element.88) | copy-start | bytes 393220
  259.2 23.1 %copy-start.81 = (bf16[512,768]{1,0:T(8,128)(2,1)S(1)}, bf16[512,768]{1,0:T(8,128)(2,1)}, u32[]{:S(2)}) copy-start(bf16[512,768]{1,0:T(8,128)(2,1)} %get-tuple-element.84) | copy-start | bytes 2359300
  282.7 9.6 %collective-permute-start.7 = (bf16[768,128]{1,0:T(8,128)(2,1)S(1)}, bf16[768,128]{1,0:T(8,128)(2,1)S(1)}, u32[]{:S(2)}, u32[]{:S(2)}) collective-permute-start(bf16[768,128]{1,0:T(8,128)(2,1)S(1)} %split.60), channel_id=1, source_target_pairs={{0,16},{16,0},{1,17},{17,1},{2,18},{18,2},{3,19},{19,3},{4,20},{20... | collective-permute-start | bytes 589832 | tf_op jit(solution)/shard_map/ppermute | solution.py:451
  283.6 12.7 %collective-permute-start.5 = (bf16[128,1536]{1,0:T(8,128)(2,1)S(1)}, bf16[128,1536]{1,0:T(8,128)(2,1)S(1)}, u32[]{:S(2)}, u32[]{:S(2)}) collective-permute-start(bf16[128,1536]{1,0:T(8,128)(2,1)S(1)} %pad_maximum_fusion.6), channel_id=1, source_target_pairs={{0,16},{16,0},{1,17},{17,1},{2,18},{18,2},{3,19},{19,3},{4,20},{20... | collective-permute-start | bytes 1179656 | tf_op jit(solution)/shard_map/ppermute | solution.py:455
  284.1 5.7 %collective-permute-start.3 = (bf16[512,128]{1,0:T(8,128)(2,1)S(1)}, bf16[512,128]{1,0:T(8,128)(2,1)S(1)}, u32[]{:S(2)}, u32[]{:S(2)}) collective-permute-start(bf16[512,128]{1,0:T(8,128)(2,1)S(1)} %split.62), channel_id=1, source_target_pairs={{0,16},{16,0},{1,17},{17,1},{2,18},{18,2},{3,19},{19,3},{4,20},{20... | collective-permute-start | bytes 393224 | tf_op jit(solution)/shard_map/ppermute | solution.py:451
  284.8 8.9 %collective-permute-start.1 = (bf16[128,1024]{1,0:T(8,128)(2,1)S(1)}, bf16[128,1024]{1,0:T(8,128)(2,1)S(1)}, u32[]{:S(2)}, u32[]{:S(2)}) collective-permute-start(bf16[128,1024]{1,0:T(8,128)(2,1)S(1)} %pad_maximum_fusion.12), channel_id=1, source_target_pairs={{0,16},{16,0},{1,17},{17,1},{2,18},{18,2},{3,19},{19,3},{4,20},{20... | collective-permute-start | bytes 786440 | tf_op jit(solution)/shard_map/ppermute | solution.py:455
  285.5 7.2 %collective-permute-start.6 = (bf16[768,128]{1,0:T(8,128)(2,1)S(1)}, bf16[768,128]{1,0:T(8,128)(2,1)S(1)}, u32[]{:S(2)}, u32[]{:S(2)}) collective-permute-start(bf16[768,128]{1,0:T(8,128)(2,1)S(1)} %split.61), channel_id=1, source_target_pairs={{0,16},{16,0},{1,17},{17,1},{2,18},{18,2},{3,19},{19,3},{4,20},{20... | collective-permute-start | bytes 589832 | tf_op jit(solution)/shard_map/ppermute | solution.py:451
  289.9 1.4 collective-permute-start.2
  291.3 5.2 %collective-permute-start.4 = (bf16[128,1536]{1,0:T(8,128)(2,1)S(1)}, bf16[128,1536]{1,0:T(8,128)(2,1)S(1)}, u32[]{:S(2)}, u32[]{:S(2)}) collective-permute-start(bf16[128,1536]{1,0:T(8,128)(2,1)S(1)} %pad_maximum_fusion.5), channel_id=1, source_target_pairs={{0,16},{16,0},{1,17},{17,1},{2,18},{18,2},{3,19},{19,3},{4,20},{20... | collective-permute-start | bytes 1179656 | tf_op jit(solution)/shard_map/ppermute | solution.py:455
  292.4 1.5 collective-permute-start
  296.7 8.9 %copy-start.11 = (f32[32,1024]{1,0:T(8,128)S(1)}, f32[32,1024]{1,0:T(8,128)}, u32[]{:S(2)}) copy-start(f32[32,1024]{1,0:T(8,128)} %copy-done.9) | copy-start | bytes 393220
  (62 other events, 105.8 us)
Sparse Core Ops, SparseCore 0:
  11.3 59.4 all-gather.1
  282.3 23.2 reduce-scatter.1

commit v3 on v2

--- a/solution.py
+++ b/solution.py
@@ -65,15 +65,11 @@
     tp_peers = [lax.rem(me_t + d, n_tp) for d in range(1, n_tp)]
     ctx_peers = [lax.rem(me_c + d, n_ctx) for d in range(1, n_ctx)] if has_gather else []
     barrier = pltpu.get_barrier_semaphore()
-    side = me_t + 1 - 2 * lax.rem(me_t, 2)
-    over = lax.rem(me_t + 2, n_tp)
-    cross = lax.rem(side + 2, n_tp)
-    greeted = tp_peers if has_sum else [side, over]
-    for peer in greeted:
+    for peer in tp_peers:
         pl.semaphore_signal(barrier, inc=1, device_id={"tp": peer}, device_id_type=MESH)
     for peer in ctx_peers:
         pl.semaphore_signal(barrier, inc=1, device_id={"ctx": peer}, device_id_type=MESH)
-    pl.semaphore_wait(barrier, len(greeted) + len(ctx_peers))
+    pl.semaphore_wait(barrier, len(tp_peers) + len(ctx_peers))
 
     if has_sum:
         sums = [
@@ -106,54 +102,33 @@
 
     if has_gather:
         own[...] = sent
-        half = own.shape[0] // 2
-        order = sorted(range(1, n_ctx), key=lambda d: min(2 * d - 1, 2 * (n_ctx - d)))
         copies = []
-        for d in order:
-            peer = ctx_peers[d - 1]
+        for d, peer in enumerate(ctx_peers):
             copies.append(
+                remote(own, out.at[me_c, me_t], z_send.at[d], z_recv.at[d], ctx=peer)
+            )
+        for d, peer in enumerate(tp_peers):
+            copies.append(
+                remote(own, out.at[me_c, me_t], t_send.at[0, d], t_recv.at[0, d], tp=peer)
+            )
+        for copy in copies:
+            copy.start()
+        out[me_c, me_t] = sent
+        for d in range(n_ctx - 1):
+            source = lax.rem(me_c + n_ctx - (d + 1), n_ctx)
+            slot = out.at[source, me_t]
+            remote(own, slot, z_send.at[d], z_recv.at[d], ctx=source).wait_recv()
+            for k, peer in enumerate(tp_peers):
+                copy = remote(slot, slot, t_send.at[d + 1, k], t_recv.at[d + 1, k], tp=peer)
+                copy.start()
+                copies.append(copy)
+        for d in range(n_ctx):
+            source = lax.rem(me_c + n_ctx - d, n_ctx)
+            for k in range(n_tp - 1):
+                origin = lax.rem(me_t + n_tp - (k + 1), n_tp)
                 remote(
-                    own, out.at[me_c, me_t], z_send.at[d - 1], z_recv.at[d - 1], ctx=peer
-                )
-            )
-            copies[-1].start()
-
-        def place(d, origin):
-            return out.at[lax.rem(me_c + n_ctx - d, n_ctx), origin]
-
-        def send(src, dst, d, k, peer):
-            copies.append(remote(src, dst, t_send.at[d, k], t_recv.at[d, k], tp=peer))
-            copies[-1].start()
-
-        def arrive(dst, d, k, peer):
-            remote(dst, dst, t_send.at[d, k], t_recv.at[d, k], tp=peer).wait_recv()
-
-        def spread(d):
-            src = own if d == 0 else place(d, me_t)
-            send(src, place(d, me_t), d, 0, side)
-            send(src, place(d, me_t), d, 1, over)
-
-        def relay(d):
-            arrive(place(d, side), d, 0, side)
-            upper = place(d, side).at[pl.ds(0, half)]
-            send(upper, upper, d, 2, over)
-            arrive(place(d, over), d, 1, over)
-            lower = place(d, over).at[pl.ds(half, half)]
-            send(lower, lower, d, 3, side)
-
-        spread(0)
-        out[me_c, me_t] = sent
-        behind = 0
-        for d in order:
-            source = lax.rem(me_c + n_ctx - d, n_ctx)
-            remote(own, place(d, me_t), z_send.at[d - 1], z_recv.at[d - 1], ctx=source).wait_recv()
-            spread(d)
-            relay(behind)
-            behind = d
-        relay(behind)
-        for d in [0] + order:
-            arrive(place(d, cross).at[pl.ds(0, half)], d, 2, over)
-            arrive(place(d, cross).at[pl.ds(half, half)], d, 3, side)
+                    own, out.at[source, origin], t_send.at[d, k], t_recv.at[d, k], tp=origin
+                ).wait_recv()
         for copy in copies:
             copy.wait_send()
 
@@ -187,8 +162,8 @@
             pltpu.VMEM((rows, width), BF16),
             dma((n_ctx - 1,)),
             dma((n_ctx - 1,)),
-            dma((n_ctx, 4)),
-            dma((n_ctx, 4)),
+            dma((n_ctx, n_tp - 1)),
+            dma((n_ctx, n_tp - 1)),
         ]
     vmem = pl.BlockSpec(memory_space=pltpu.VMEM)
     outs = pl.pallas_call(
@@ -423,7 +398,7 @@
     grad_output,
 ):
     local_rows, seq_local, width = block_input.shape
-    assert seq_local == 1 and lax.axis_size("dp") == 2 and lax.axis_size("tp") == 4
+    assert seq_local == 1 and lax.axis_size("dp") == 2
     layers = input_gain.shape[0]
     head_dim = query_gain.shape[-1]
     heads = query_weight.shape[-1] // head_dim

time: 315 us -> 301 us (0.956)
  Pallas kernels: 205 us -> 191 us
    pallas_call x8, Pallas kernels: 157 us -> 142 us  [boundary(): pl.pallas_call(functools.partial(boundary_kernel, mode, n_ctx, n_tp), out...]
  transfers between devices with their start and end apart: 10 -> 10, of which waited for: 3 -> 3; matrix products, arithmetic and copies ran while one was open for 11% -> 11% of each run, Pallas kernels for 32% -> 31%
where the time goes in v3:
time: 301 us; the launch traced here: 300 us
  Pallas kernels  191 us (63%)
  matrix products  43.6 us (14%)
  local copies, waits for them, and re-layouts  26.6 us (9%)
  between operations  15.3 us (5%)
  other arithmetic  13 us (4%)
  waiting for transfers between devices  8.26 us (3%)
    pallas_call x8, Pallas kernels, boundary(): pl.pallas_call(functools.partial(boundary_kernel, mode, n_ctx, n_tp), out...  142 us
    dot_general x42, matrix products, dot(): return lax.dot_general(a, b, dims, preferred_element_type=F32)  43.6 us
    pallas_call x4, Pallas kernels, attention(): pl.pallas_call(functools.partial(attend_back_kernel if back else attend_k...  36.7 us
    unnamed x176, local copies, waits for them, and re-layouts  13.9 us
    pallas_call x1, Pallas kernels, sum_gains(): pl.pallas_call(functools.partial(gains_kernel, sizes), out_shape=jax.Shap...  11.9 us
    dynamic_slice x7, local copies, waits for them, and re-layouts, slices(): lax.dynamic_slice_in_dim(x, at, piece, 1)  7.65 us
    reduce_scatter x1, waiting for transfers between devices, on_device(): lax.psum_scatter(partial, 'tp', scatter_dimension=0, tiled=True).astype(F32)  7.04 us
    another operation x17, other arithmetic, on_device(): stacked = [jnp.stack([part[m] for part in grads]) for m in range(7)]  6.36 us
  transfers between devices with their start and end apart: 10, of which 3 were waited for; matrix products, arithmetic and copies ran while one was open for 11% of the time, Pallas kernels for 31%

profile of v3, /device:TPU:0, one launch (start us, length us, event | category | flops | bytes accessed | tf_op | source)
XLA Modules:
  0.0 299.6 jit_solution(941194305385545642)
XLA Ops:
  7.2 1.6 copy.48
  11.5 1.7 fusion.146
  13.2 19.8 %boundary_first.1 = bf16[4,4,32,1024]{3,2,1,0:T(8,128)(2,1)S(1)} custom-call(f32[32,1024]{1,0:T(8,128)S(1)} %bitcast.188, f32[1,1024]{1,0:T(1,128)S(1)} %get-tuple-element.120.refs_1_.refs_2_), custom_call_target="tpu_custom_call" | custom-call | tf_op jit(solution)/shard_map/boundary_first/pallas_call | solution.py:169
  36.6 1.4 pad_maximum_fusion.7
  38.0 6.2 %attend.2.o_ref = bf16[512,512]{1,0:T(8,128)(2,1)S(1)} custom-call(f32[512,512]{1,0:T(8,128)S(1)} %fusion.68.q_ref, f32[512,256]{1,0:T(8,128)S(1)} %copy-done.5, bf16[512,256]{1,0:T(8,128)(2,1)S(1)} %convolution_convert_fusion.5.v_ref, f32[512,128]{1,0:T(8,128)S(1)} %get-tuple-element.130.cq_ref.ck_ref, f32[512,128]{1,0:T(8,128)S(1)} %get-tuple-element.131.sq_ref.sk_ref, ...), custom_call_target="tpu_custom_call" | custom-call | flops 536870912 | bytes 2097152 | tf_op jit(solution)/shard_map/attend/pallas_call | solution.py:358
  44.6 22.7 %boundary_fwd.3 = (f32[32,1024]{1,0:T(8,128)S(1)}, bf16[4,4,32,1024]{3,2,1,0:T(8,128)(2,1)S(1)}) custom-call(bf16[4,32,1024]{2,1,0:T(8,128)(2,1)S(1)} %bitcast.202, f32[32,1024]{1,0:T(8,128)S(1)} %bitcast.189, f32[1,1024]{1,0:T(1,128)S(1)} %get-tuple-element.118.refs_2_), custom_call_target="tpu_custom_call" | custom-call | tf_op jit(solution)/shard_map/boundary_fwd/pallas_call | solution.py:169
  68.3 1.3 copy-done.29
  69.6 2.2 multiply_convert_fusion.5
  75.4 18.9 %boundary_fwd.4 = (f32[32,1024]{1,0:T(8,128)S(1)}, bf16[4,4,32,1024]{3,2,1,0:T(8,128)(2,1)S(1)}) custom-call(bf16[4,32,1024]{2,1,0:T(8,128)(2,1)S(1)} %bitcast.200, f32[32,1024]{1,0:T(8,128)S(1)} %get-tuple-element.41.refs_1_, f32[1,1024]{1,0:T(1,128)S(1)} %get-tuple-element.119.refs_2_), custom_call_target="tpu_custom_call" | custom-call | tf_op jit(solution)/shard_map/boundary_fwd/pallas_call | solution.py:169
  94.3 1.5 convolution_convert_fusion.3.v_ref
  98.3 6.4 %attend.3.o_ref = bf16[512,512]{1,0:T(8,128)(2,1)S(1)} custom-call(f32[512,512]{1,0:T(8,128)S(1)} %fusion.63.q_ref, f32[512,256]{1,0:T(8,128)S(1)} %fusion.83.k_ref, bf16[512,256]{1,0:T(8,128)(2,1)S(1)} %convolution_convert_fusion.3.v_ref, f32[512,128]{1,0:T(8,128)S(1)} %get-tuple-element.130.cq_ref.ck_ref, f32[512,128]{1,0:T(8,128)S(1)} %get-tuple-element.131.sq_ref.sk_ref, ...), custom_call_target="tpu_custom_call" | custom-call | flops 536870912 | bytes 2097152 | tf_op jit(solution)/shard_map/attend/pallas_call | solution.py:358
  105.1 19.4 %boundary_fwd.5 = (f32[32,1024]{1,0:T(8,128)S(1)}, bf16[4,4,32,1024]{3,2,1,0:T(8,128)(2,1)S(1)}) custom-call(bf16[4,32,1024]{2,1,0:T(8,128)(2,1)S(1)} %bitcast.201, f32[32,1024]{1,0:T(8,128)S(1)} %get-tuple-element.43.refs_1_, f32[1,1024]{1,0:T(1,128)S(1)} %get-tuple-element.117.refs_2_), custom_call_target="tpu_custom_call" | custom-call | tf_op jit(solution)/shard_map/boundary_fwd/pallas_call | solution.py:169
  125.2 2.0 constant_dynamic-slice_fusion.7
  128.8 2.2 fusion.6
  130.9 2.9 fusion
  133.9 4.0 %multiply_convert_fusion.3 = (bf16[512,768]{1,0:T(8,128)(2,1)S(1)}, bf16[512,768]{1,0:T(8,128)(2,1)S(1)}, bf16[512,768]{1,0:T(8,128)(2,1)}) fusion(f32[512,768]{1,0:T(8,128)S(1)} %fusion, f32[512,768]{1,0:T(8,128)} %fusion.6, bf16[512,1024]{1,0:T(8,128)(2,1)S(1)} %bitcast.209, bf16[2,1024,768]{2,1,0:T(8,128)(2,1)S(1)} %copy-done.33), kind=kOutput, calls=%fused_computation.27 | convolution fusion | flops 811204608 | bytes 8126464 | tf_op jit(solution)/shard_map/dot_general | solution.py:250
  138.9 1.3 fusion.134
  140.2 1.3 fusion.135
  142.4 17.8 %boundary_bwd.3 = (f32[32,1024]{1,0:T(8,128)S(1)}, f32[1,1024]{1,0:T(1,128)S(1)}, bf16[4,4,32,1024]{3,2,1,0:T(8,128)(2,1)S(1)}) custom-call(bf16[4,32,1024]{2,1,0:T(8,128)(2,1)S(1)} %bitcast.196, f32[32,1024]{1,0:T(8,128)S(1)} %copy-done.10, f32[1,1024]{1,0:T(1,128)S(1)} %get-tuple-element.117.refs_2_, f32[32,1024]{1,0:T(8,128)S(1)} %bitcast.199), custom_call_target="tpu_custom_call" | custom-call | tf_op jit(solution)/shard_map/boundary_bwd/pallas_call | solution.py:169
  162.6 12.0 %attend_back.2 = (bf16[512,512]{1,0:T(8,128)(2,1)S(1)}, bf16[512,256]{1,0:T(8,128)(2,1)S(1)}, bf16[512,256]{1,0:T(8,128)(2,1)S(1)}, f32[1,128]{1,0:T(1,128)S(1)}, f32[1,128]{1,0:T(1,128)S(1)}) custom-call(f32[512,512]{1,0:T(8,128)S(1)} %copy-done.1, f32[512,256]{1,0:T(8,128)S(1)} %copy-done.8, bf16[512,256]{1,0:T(8,128)(2,1)S(1)} %copy-done.16, ...), custom_call_target="tpu_custom_call" | custom-call | flops 1342177280 | bytes 2097152 | tf_op jit(solution)/shard_map/attend_back/pallas_call | solution.py:358
  178.9 19.6 %boundary_bwd.4 = (f32[32,1024]{1,0:T(8,128)S(1)}, f32[1,1024]{1,0:T(1,128)S(1)}, bf16[4,4,32,1024]{3,2,1,0:T(8,128)(2,1)S(1)}) custom-call(bf16[4,32,1024]{2,1,0:T(8,128)(2,1)S(1)} %bitcast.195, f32[32,1024]{1,0:T(8,128)S(1)} %get-tuple-element.43.refs_1_, f32[1,1024]{1,0:T(1,128)S(1)} %get-tuple-element.119.refs_2_, f32[32,1024]{1,0:T(8,128)S(1)} %get-tuple-element.50.refs_3_), custom_call_target="tpu_custom_call" | custom-call | tf_op jit(solution)/shard_map/boundary_bwd/pallas_call | solution.py:169
  199.3 2.9 multiply_convert_fusion.1
  203.1 1.3 fusion.136
  204.5 1.4 fusion.137
  206.5 17.8 %boundary_bwd.5 = (f32[32,1024]{1,0:T(8,128)S(1)}, f32[1,1024]{1,0:T(1,128)S(1)}, bf16[4,4,32,1024]{3,2,1,0:T(8,128)(2,1)S(1)}) custom-call(bf16[4,32,1024]{2,1,0:T(8,128)(2,1)S(1)} %bitcast.197, f32[32,1024]{1,0:T(8,128)S(1)} %get-tuple-element.41.refs_1_, f32[1,1024]{1,0:T(1,128)S(1)} %get-tuple-element.118.refs_2_, f32[32,1024]{1,0:T(8,128)S(1)} %get-tuple-element.52.refs_3_), custom_call_target="tpu_custom_call" | custom-call | tf_op jit(solution)/shard_map/boundary_bwd/pallas_call | solution.py:169
  226.2 12.0 %attend_back.3 = (bf16[512,512]{1,0:T(8,128)(2,1)S(1)}, bf16[512,256]{1,0:T(8,128)(2,1)S(1)}, bf16[512,256]{1,0:T(8,128)(2,1)S(1)}, f32[1,128]{1,0:T(1,128)S(1)}, f32[1,128]{1,0:T(1,128)S(1)}) custom-call(f32[512,512]{1,0:T(8,128)S(1)} %fusion.68.q_ref, f32[512,256]{1,0:T(8,128)S(1)} %copy-done.6, bf16[512,256]{1,0:T(8,128)(2,1)S(1)} %copy-done.14, ...), custom_call_target="tpu_custom_call" | custom-call | flops 1342177280 | bytes 2097152 | tf_op jit(solution)/shard_map/attend_back/pallas_call | solution.py:358
  238.6 1.8 constant_dynamic-slice_fusion.1
  244.2 6.1 %boundary_bwd_last.1 = (f32[32,1024]{1,0:T(8,128)S(1)}, f32[1,1024]{1,0:T(1,128)S(1)}) custom-call(bf16[4,32,1024]{2,1,0:T(8,128)(2,1)S(1)} %bitcast.198, f32[32,1024]{1,0:T(8,128)S(1)} %bitcast.190, f32[1,1024]{1,0:T(1,128)S(1)} %get-tuple-element.120.refs_1_.refs_2_, f32[32,1024]{1,0:T(8,128)S(1)} %get-tuple-element.57.refs_3_), custom_call_target="tpu_custom_call" | custom-call | tf_op jit(solution)/shard_map/boundary_bwd_last/pallas_call | solution.py:169
  251.0 11.9 %sum_gains.1 = f32[40,128]{1,0:T(8,128)} custom-call(f32[40,128]{1,0:T(8,128)} %pad_bitcast_fusion.x_ref), custom_call_target="tpu_custom_call" | custom-call | tf_op jit(solution)/shard_map/sum_gains/pallas_call | solution.py:231
  262.9 1.3 fusion.187
  265.1 2.6 fusion.57
  284.1 7.0 %reduce-scatter.2.cloned.1.call-done = bf16[32,1024]{1,0:T(8,128)(2,1)} async-done(((bf16[128,1024]{1,0:T(8,128)(2,1)}), bf16[32,1024]{1,0:T(8,128)(2,1)}) %reduce-scatter.2.cloned.1.call-update) | async-done | bytes 65552 | tf_op jit(solution)/shard_map/reduce_scatter | solution.py:462
  (286 shorter events, 52.0 us)
Async XLA Ops:
  7.2 25.8 %copy-start.47 = (bf16[2,1024,256]{2,1,0:T(8,128)(2,1)S(1)}, bf16[2,1024,256]{2,1,0:T(8,128)(2,1)}, u32[]{:S(2)}) copy-start(bf16[2,1024,256]{2,1,0:T(8,128)(2,1)} %param.17) | copy-start | bytes 3145732
  7.2 123.8 %all-gather.2.cloned.1.call-start = ((), (), s32[]{:S(2)}) async-start(), calls=%async_computation.2 | async-start | bytes 1114112 | tf_op jit(solution)/shard_map/all_gather | solution.py:440
  8.9 282.2 %reduce-scatter.2.cloned.1.call-start = ((), (), s32[]{:S(2)}) async-start(), calls=%async_computation.1 | async-start | bytes 327680 | tf_op jit(solution)/shard_map/reduce_scatter | solution.py:462
  13.2 20.2 %copy-start.49 = (bf16[2,1024,256]{2,1,0:T(8,128)(2,1)S(1)}, bf16[2,1024,256]{2,1,0:T(8,128)(2,1)}, u32[]{:S(2)}) copy-start(bf16[2,1024,256]{2,1,0:T(8,128)(2,1)} %param.16) | copy-start | bytes 3145732
  36.6 7.7 %copy-start.21 = (f32[1,128]{1,0:T(1,128)}, f32[1,128]{1,0:T(1,128)S(1)}, u32[]{:S(2)}) copy-start(f32[1,128]{1,0:T(1,128)S(1)} %get-tuple-element.122.kg_ref) | copy-start | bytes 1540
  36.6 7.7 %copy-start.23 = (f32[1,128]{1,0:T(1,128)}, f32[1,128]{1,0:T(1,128)S(1)}, u32[]{:S(2)}) copy-start(f32[1,128]{1,0:T(1,128)S(1)} %get-tuple-element.132.qg_ref) | copy-start | bytes 1540
  36.6 7.7 %copy-start.75 = (bf16[2,512,1024]{2,1,0:T(8,128)(2,1)S(1)}, bf16[2,512,1024]{2,1,0:T(8,128)(2,1)}, u32[]{:S(2)}) copy-start(bf16[2,512,1024]{2,1,0:T(8,128)(2,1)} %param.20) | copy-start | bytes 6291460
  38.0 29.4 %copy-start.32 = (bf16[2,1024,768]{2,1,0:T(8,128)(2,1)S(1)}, bf16[2,1024,768]{2,1,0:T(8,128)(2,1)}, u32[]{:S(2)}) copy-start(bf16[2,1024,768]{2,1,0:T(8,128)(2,1)} %param.22) | copy-start | bytes 9437188
  75.4 20.4 %copy-start.50 = (bf16[2,1024,256]{2,1,0:T(8,128)(2,1)S(1)}, bf16[2,1024,256]{2,1,0:T(8,128)(2,1)}, u32[]{:S(2)}) copy-start(bf16[2,1024,256]{2,1,0:T(8,128)(2,1)} %param.16) | copy-start | bytes 3145732
  98.2 6.5 %copy-start = (f32[512,512]{1,0:T(8,128)}, f32[512,512]{1,0:T(8,128)S(1)}, u32[]{:S(2)}) copy-start(f32[512,512]{1,0:T(8,128)S(1)} %fusion.63.q_ref) | copy-start | bytes 3145732
  98.3 6.4 %copy-start.76 = (bf16[2,512,1024]{2,1,0:T(8,128)(2,1)S(1)}, bf16[2,512,1024]{2,1,0:T(8,128)(2,1)}, u32[]{:S(2)}) copy-start(bf16[2,512,1024]{2,1,0:T(8,128)(2,1)} %param.20) | copy-start | bytes 6291460
  104.8 24.0 %copy-start.2 = (bf16[512,512]{1,0:T(8,128)(2,1)}, bf16[512,512]{1,0:T(8,128)(2,1)S(1)}, u32[]{:S(2)}) copy-start(bf16[512,512]{1,0:T(8,128)(2,1)S(1)} %attend.3.o_ref) | copy-start | bytes 1572868
  104.8 24.0 %copy-start.30 = (bf16[2,1024,768]{2,1,0:T(8,128)(2,1)S(1)}, bf16[2,1024,768]{2,1,0:T(8,128)(2,1)}, u32[]{:S(2)}) copy-start(bf16[2,1024,768]{2,1,0:T(8,128)(2,1)} %param.23) | copy-start | bytes 9437188
  141.5 19.5 %copy-start.77 = (bf16[2,512,1024]{2,1,0:T(8,128)(2,1)S(1)}, bf16[2,512,1024]{2,1,0:T(8,128)(2,1)}, u32[]{:S(2)}) copy-start(bf16[2,512,1024]{2,1,0:T(8,128)(2,1)} %param.20) | copy-start | bytes 6291460
  162.6 12.1 %copy-start.48 = (bf16[2,1024,256]{2,1,0:T(8,128)(2,1)S(1)}, bf16[2,1024,256]{2,1,0:T(8,128)(2,1)}, u32[]{:S(2)}) copy-start(bf16[2,1024,256]{2,1,0:T(8,128)(2,1)} %param.17) | copy-start | bytes 3145732
  162.6 12.4 %copy-start.53 = (bf16[512,128]{1,0:T(8,128)(2,1)S(1)}, bf16[512,128]{1,0:T(8,128)(2,1)}, u32[]{:S(2)}) copy-start(bf16[512,128]{1,0:T(8,128)(2,1)} %get-tuple-element.99) | copy-start | bytes 393220
  162.6 12.4 %copy-start.54 = (bf16[512,128]{1,0:T(8,128)(2,1)S(1)}, bf16[512,128]{1,0:T(8,128)(2,1)}, u32[]{:S(2)}) copy-start(bf16[512,128]{1,0:T(8,128)(2,1)} %get-tuple-element.100) | copy-start | bytes 393220
  177.3 22.0 %copy-start.83 = (f32[512,768]{1,0:T(8,128)S(1)}, f32[512,768]{1,0:T(8,128)}, u32[]{:S(2)}) copy-start(f32[512,768]{1,0:T(8,128)} %copy-done.82) | copy-start | bytes 4718596
  178.4 20.9 %copy-start.74 = (bf16[2,768,1024]{2,1,0:T(8,128)(2,1)S(1)}, bf16[2,768,1024]{2,1,0:T(8,128)(2,1)}, u32[]{:S(2)}) copy-start(bf16[2,768,1024]{2,1,0:T(8,128)(2,1)} %param.24) | copy-start | bytes 9437188
  205.8 19.3 %copy-start.78 = (bf16[2,512,1024]{2,1,0:T(8,128)(2,1)S(1)}, bf16[2,512,1024]{2,1,0:T(8,128)(2,1)}, u32[]{:S(2)}) copy-start(bf16[2,512,1024]{2,1,0:T(8,128)(2,1)} %param.20) | copy-start | bytes 6291460
  244.2 23.5 %copy-start.59 = (bf16[512,128]{1,0:T(8,128)(2,1)S(1)}, bf16[512,128]{1,0:T(8,128)(2,1)}, u32[]{:S(2)}) copy-start(bf16[512,128]{1,0:T(8,128)(2,1)} %get-tuple-element.87) | copy-start | bytes 393220
  244.2 23.5 %copy-start.60 = (bf16[512,128]{1,0:T(8,128)(2,1)S(1)}, bf16[512,128]{1,0:T(8,128)(2,1)}, u32[]{:S(2)}) copy-start(bf16[512,128]{1,0:T(8,128)(2,1)} %get-tuple-element.88) | copy-start | bytes 393220
  244.2 23.5 %copy-start.81 = (bf16[512,768]{1,0:T(8,128)(2,1)S(1)}, bf16[512,768]{1,0:T(8,128)(2,1)}, u32[]{:S(2)}) copy-start(bf16[512,768]{1,0:T(8,128)(2,1)} %get-tuple-element.84) | copy-start | bytes 2359300
  268.2 9.6 %collective-permute-start.7 = (bf16[768,128]{1,0:T(8,128)(2,1)S(1)}, bf16[768,128]{1,0:T(8,128)(2,1)S(1)}, u32[]{:S(2)}, u32[]{:S(2)}) collective-permute-start(bf16[768,128]{1,0:T(8,128)(2,1)S(1)} %split.60), channel_id=1, source_target_pairs={{0,16},{16,0},{1,17},{17,1},{2,18},{18,2},{3,19},{19,3},{4,20},{20... | collective-permute-start | bytes 589832 | tf_op jit(solution)/shard_map/ppermute | solution.py:426
  269.1 12.7 %collective-permute-start.5 = (bf16[128,1536]{1,0:T(8,128)(2,1)S(1)}, bf16[128,1536]{1,0:T(8,128)(2,1)S(1)}, u32[]{:S(2)}, u32[]{:S(2)}) collective-permute-start(bf16[128,1536]{1,0:T(8,128)(2,1)S(1)} %pad_maximum_fusion.6), channel_id=1, source_target_pairs={{0,16},{16,0},{1,17},{17,1},{2,18},{18,2},{3,19},{19,3},{4,20},{20... | collective-permute-start | bytes 1179656 | tf_op jit(solution)/shard_map/ppermute | solution.py:430
  269.6 5.7 %collective-permute-start.3 = (bf16[512,128]{1,0:T(8,128)(2,1)S(1)}, bf16[512,128]{1,0:T(8,128)(2,1)S(1)}, u32[]{:S(2)}, u32[]{:S(2)}) collective-permute-start(bf16[512,128]{1,0:T(8,128)(2,1)S(1)} %split.62), channel_id=1, source_target_pairs={{0,16},{16,0},{1,17},{17,1},{2,18},{18,2},{3,19},{19,3},{4,20},{20... | collective-permute-start | bytes 393224 | tf_op jit(solution)/shard_map/ppermute | solution.py:426
  270.3 8.9 %collective-permute-start.1 = (bf16[128,1024]{1,0:T(8,128)(2,1)S(1)}, bf16[128,1024]{1,0:T(8,128)(2,1)S(1)}, u32[]{:S(2)}, u32[]{:S(2)}) collective-permute-start(bf16[128,1024]{1,0:T(8,128)(2,1)S(1)} %pad_maximum_fusion.12), channel_id=1, source_target_pairs={{0,16},{16,0},{1,17},{17,1},{2,18},{18,2},{3,19},{19,3},{4,20},{20... | collective-permute-start | bytes 786440 | tf_op jit(solution)/shard_map/ppermute | solution.py:430
  271.0 7.2 %collective-permute-start.6 = (bf16[768,128]{1,0:T(8,128)(2,1)S(1)}, bf16[768,128]{1,0:T(8,128)(2,1)S(1)}, u32[]{:S(2)}, u32[]{:S(2)}) collective-permute-start(bf16[768,128]{1,0:T(8,128)(2,1)S(1)} %split.61), channel_id=1, source_target_pairs={{0,16},{16,0},{1,17},{17,1},{2,18},{18,2},{3,19},{19,3},{4,20},{20... | collective-permute-start | bytes 589832 | tf_op jit(solution)/shard_map/ppermute | solution.py:426
  275.4 1.4 collective-permute-start.2
  276.8 5.2 %collective-permute-start.4 = (bf16[128,1536]{1,0:T(8,128)(2,1)S(1)}, bf16[128,1536]{1,0:T(8,128)(2,1)S(1)}, u32[]{:S(2)}, u32[]{:S(2)}) collective-permute-start(bf16[128,1536]{1,0:T(8,128)(2,1)S(1)} %pad_maximum_fusion.5), channel_id=1, source_target_pairs={{0,16},{16,0},{1,17},{17,1},{2,18},{18,2},{3,19},{19,3},{4,20},{20... | collective-permute-start | bytes 1179656 | tf_op jit(solution)/shard_map/ppermute | solution.py:430
  277.9 1.5 collective-permute-start
  282.2 8.9 %copy-start.11 = (f32[32,1024]{1,0:T(8,128)S(1)}, f32[32,1024]{1,0:T(8,128)}, u32[]{:S(2)}) copy-start(f32[32,1024]{1,0:T(8,128)} %copy-done.9) | copy-start | bytes 393220
  (62 other events, 105.8 us)
Sparse Core Ops, SparseCore 0:
  11.3 60.7 all-gather.1
  267.8 23.2 reduce-scatter.1
